TPU v7x, 32 devices: a whole 2x2x4 slice. The times are simulated.
32 devices in a mesh: fsdp: 4 (over y, x), context: 4 (over z), tensor: 2 (over core).
Axes of the slice: x: 2, y: 2, z: 4, core: 2. Of those that a mesh axis runs over, the one named last changes fastest.
Arguments:
- tokens: bfloat16 [12288, 768], P(('fsdp', 'context')), may hold values from -6 to 6
- cotangent: bfloat16 [12288, 768], P(('fsdp', 'context')), may hold values from -6 to 6
- w_qkv: bfloat16 [3, 768, 768], P(None, 'fsdp', 'tensor'), may hold values from -0.21875 to 0.21875
- bias_qv: float32 [2, 768], P(None, 'tensor'), may hold values from -3 to 3
- w_attn_out: bfloat16 [768, 768], P('tensor', 'fsdp'), may hold values from -1.25 to 1.25
- w_up: bfloat16 [768, 3072], P('fsdp', 'tensor'), may hold values from -0.21875 to 0.21875
- bias_up: float32 [3072], P('tensor'), may hold values from -3 to 3
- w_down: bfloat16 [3072, 768], P('tensor', 'fsdp'), may hold values from -0.109375 to 0.109375
- gains: float32 [2, 768], replicated, may hold values from 0.1 to 1.9
- shifts: float32 [4, 768], replicated, may hold values from -3 to 3
- seq_lengths: int32 [4, 3], P('fsdp'), may hold values from 1 to 1536, 3072 in all within a row
- key_mask: int32 [12288], P('fsdp'), may hold values 0 or 1
Outputs:
- out: bfloat16 [12288, 768], P(('fsdp', 'context'))
- grad_tokens: bfloat16 [12288, 768], P(('fsdp', 'context'))
- grad_qkv: float32 [3, 768, 768], P(None, 'fsdp', 'tensor')
- grad_attn_out: float32 [768, 768], P('tensor', 'fsdp')
- grad_up: float32 [768, 3072], P('fsdp', 'tensor')
- grad_down: float32 [3072, 768], P('tensor', 'fsdp')
- grad_bias_qv: float32 [2, 768], P(None, 'tensor')
- grad_bias_up: float32 [3072], P('tensor')
- grad_gains: float32 [2, 768], replicated
- grad_shifts: float32 [4, 768], replicated
Inputs may be any that keep to these rules, and one draw needn't show every extreme that they name: `seq_lengths`: row f holds the lengths of the 3 sequences packed in order into the 3072 rows of group f; they sum to 3072 and the longest is 1536 in every row. `key_mask`: 1 marks a row that other rows of its sequence attend to; every row attends to itself.
All inputs are finite; a program needn't handle non-finite values. No bound on the sum of `key_mask` on one device may be relied on, other than what follows from the above.
Results may differ from a plain program's by a relative error of at most 0.022.
Values may be sent and summed in bfloat16 or wider, within the bound.
No kernel may reach another device: no remote copies, remote signals or barrier semaphores. Data moves between devices by JAX's collectives and lax.ppermute only.
A program may use at most 192 MiB of HBM per device.

v0:
```python
import jax
import jax.numpy as jnp
import numpy as np
from jax import lax
from jax.experimental import pallas as pl
from jax.experimental.pallas import tpu as pltpu
from jax.sharding import PartitionSpec as P

EPSILON = 1e-12
LOG2E = 1.4426950408889634
NEG = -1e30
BQ = 256
BK = 256
F32 = jnp.float32
BF16 = jnp.bfloat16
ROW = (((1,), (1,)), ((), ()))
COL = (((1,), (0,)), ((), ()))
LIMIT = 56 * 1024 * 1024
COST = pl.CostEstimate(flops=36_000_000_000, transcendentals=0, bytes_accessed=8_000_000)
PAIR_COST = pl.CostEstimate(flops=14_000_000_000, transcendentals=0, bytes_accessed=4_000_000)


def dot(a, b, dims=COL):
    return lax.dot_general(a, b, dims, preferred_element_type=F32)


def normalize(inputs):
    center = inputs - jnp.mean(inputs, axis=-1, keepdims=True)
    factor = lax.rsqrt(jnp.mean(center * center, axis=-1, keepdims=True) + EPSILON)
    return (center * factor, factor)


def norm_back(upstream, normed, factor, gain):
    scaled = upstream * gain
    return factor * (
        scaled
        - jnp.mean(scaled, axis=-1, keepdims=True)
        - normed * jnp.mean(scaled * normed, axis=-1, keepdims=True)
    )


def segment_of(places, b1, b2):
    return (places >= b1).astype(jnp.int32) + (places >= b2).astype(jnp.int32)


def key_range(first, last, b1, b2, total):
    lo = jnp.where(first >= b2, b2, jnp.where(first >= b1, b1, 0))
    hi = jnp.where(last >= b2, total, jnp.where(last >= b1, b2, b1))
    return lo, hi


def half_mask(rows, side):
    lane = lax.broadcasted_iota(jnp.int32, (rows, 128), 1)
    return (lane < 64) if side == 0 else (lane >= 64)


def pick(pair, side):
    return jnp.where(half_mask(pair.shape[0], side), pair, jnp.zeros_like(pair))


def column(row):
    return jnp.transpose(jnp.broadcast_to(row, (128, row.shape[1])))[:, :1]


def fill_bias(bias_ref, kb_ref, first, b1, b2, j0, j1):
    cols = first + lax.broadcasted_iota(jnp.int32, (1, BQ), 1)
    col_seg = segment_of(cols, b1, b2)

    def body(j, carry):
        rows = j * BK + lax.broadcasted_iota(jnp.int32, (BK, 1), 0)
        row_seg = segment_of(rows, b1, b2)
        kept = jnp.where(rows == cols, 0.0, jnp.broadcast_to(column(kb_ref[j]), (BK, BQ)))
        bias_ref[j] = jnp.where(row_seg == col_seg, kept, NEG)
        return carry

    lax.fori_loop(j0, j1, body, 0)


def attend_kernel(s_ref, q_ref, k_ref, v_ref, kb_ref, o_ref, lset_ref, score, bias):
    total = k_ref.shape[0]
    pairs = q_ref.shape[1] // 128
    b1, b2 = s_ref[0], s_ref[1]
    first = s_ref[2] + pl.program_id(0) * BQ
    lo, hi = key_range(first, first + BQ - 1, b1, b2, total)
    j0, j1 = lo // BK, (hi + BK - 1) // BK
    fill_bias(bias, kb_ref, first, b1, b2, j0, j1)
    peaks = None
    for p in range(-1, pairs):
        nxt = p + 1
        if nxt < pairs:
            ahead = slice(nxt * 128, nxt * 128 + 128)
            heads = [pick(q_ref[:, ahead], side) for side in range(2)]
        here = slice(p * 128, p * 128 + 128)

        def body(j, carry):
            tops, tots, accs = [list(part) for part in carry]
            rows = pl.ds(pl.multiple_of(j * BK, BK), BK)
            if nxt < pairs:
                keys = k_ref[rows, ahead]
                for side in range(2):
                    s = dot(keys, heads[side], ROW) + bias[j]
                    score[nxt % 2, side, j] = s
                    tops[side] = jnp.maximum(tops[side], jnp.max(s.reshape(BK // 8, 8, BQ), axis=0))
            if p >= 0:
                turned = jnp.transpose(v_ref[rows, here])
                for side in range(2):
                    prob = jnp.exp2(score[p % 2, side, j] - peaks[side])
                    tots[side] = tots[side] + jnp.sum(prob.reshape(BK // 8, 8, BQ), axis=0)
                    accs[side] = accs[side] + dot(
                        turned[64 * side : 64 * side + 64], prob.astype(BF16)
                    )
            return (tuple(tops), tuple(tots), tuple(accs))

        low, zero, wide = jnp.full((8, BQ), NEG, F32), jnp.zeros((8, BQ), F32), jnp.zeros((64, BQ), F32)
        tops, tots, accs = lax.fori_loop(j0, j1, body, ((low, low), (zero, zero), (wide, wide)))
        if p >= 0:
            results = []
            for side in range(2):
                h = 2 * p + side
                whole = jnp.sum(tots[side], axis=0, keepdims=True)
                results.append(accs[side] * (1.0 / whole))
                lset_ref[h : h + 1, :] = peaks[side] + jnp.log2(whole)
            o_ref[:, here] = jnp.transpose(jnp.concatenate(results, axis=0)).astype(BF16)
        peaks = [jnp.max(top, axis=0, keepdims=True) for top in tops]


def attend(scalars, qkv, kb, rows, pairs):
    total = qkv.shape[0]
    width = pairs * 128
    return pl.pallas_call(
        attend_kernel,
        grid_spec=pltpu.PrefetchScalarGridSpec(
            num_scalar_prefetch=1,
            grid=(rows // BQ,),
            in_specs=[
                pl.BlockSpec((BQ, width), lambda i, s: (s[2] // BQ + i, 0)),
                pl.BlockSpec((total, width), lambda i, s: (0, 1), pipeline_mode=pl.Buffered(1)),
                pl.BlockSpec((total, width), lambda i, s: (0, 2), pipeline_mode=pl.Buffered(1)),
                pl.BlockSpec((total // BK, 1, BK), lambda i, s: (0, 0, 0)),
            ],
            out_specs=[
                pl.BlockSpec((BQ, width), lambda i, s: (i, 0)),
                pl.BlockSpec((8, BQ), lambda i, s: (0, i)),
            ],
            scratch_shapes=[
                pltpu.VMEM((2, 2, total // BK, BK, BQ), F32),
                pltpu.VMEM((total // BK, BK, BQ), F32),
            ],
        ),
        out_shape=[
            jax.ShapeDtypeStruct((rows, width), BF16),
            jax.ShapeDtypeStruct((8, rows), F32),
        ],
        compiler_params=pltpu.CompilerParams(
            dimension_semantics=("arbitrary",), vmem_limit_bytes=LIMIT
        ),
        cost_estimate=COST,
        name="attend",
    )(scalars, qkv, qkv, qkv, kb)


def query_kernel(s_ref, q_ref, k_ref, v_ref, do_ref, stat_ref, kb_ref, dq_ref, bias):
    total = k_ref.shape[0]
    pairs = q_ref.shape[1] // 128
    b1, b2 = s_ref[0], s_ref[1]
    first = s_ref[2] + pl.program_id(0) * BQ
    lo, hi = key_range(first, first + BQ - 1, b1, b2, total)
    j0, j1 = lo // BK, (hi + BK - 1) // BK
    fill_bias(bias, kb_ref, first, b1, b2, j0, j1)
    for p in range(pairs):
        span = slice(p * 128, p * 128 + 128)
        sides = []
        for side in range(2):
            h = 2 * p + side
            sides.append(
                (
                    pick(q_ref[:, span], side),
                    pick(do_ref[:, span], side),
                    stat_ref[8 + h : 9 + h, :],
                    stat_ref[h : h + 1, :],
                )
            )

        def body(j, accs):
            rows = pl.ds(pl.multiple_of(j * BK, BK), BK)
            keys = k_ref[rows, span]
            values = v_ref[rows, span]
            turned = jnp.transpose(keys)
            out = []
            for side in range(2):
                qh, gh, delta, lse = sides[side]
                prob = jnp.exp2(dot(keys, qh, ROW) + bias[j] - lse)
                score = (prob * (dot(values, gh, ROW) - delta)).astype(BF16)
                out.append(accs[side] + dot(turned[64 * side : 64 * side + 64], score))
            return tuple(out)

        zero = jnp.zeros((64, BQ), F32)
        both = lax.fori_loop(j0, j1, body, (zero, zero))
        dq_ref[:, span] = (jnp.transpose(jnp.concatenate(both, axis=0)) * 0.125).astype(BF16)


def query_grads(scalars, qkv, dout, stats, kb, rows, pairs):
    total = qkv.shape[0]
    width = pairs * 128
    return pl.pallas_call(
        query_kernel,
        grid_spec=pltpu.PrefetchScalarGridSpec(
            num_scalar_prefetch=1,
            grid=(rows // BQ,),
            in_specs=[
                pl.BlockSpec((BQ, width), lambda i, s: (s[2] // BQ + i, 0)),
                pl.BlockSpec((total, width), lambda i, s: (0, 1), pipeline_mode=pl.Buffered(1)),
                pl.BlockSpec((total, width), lambda i, s: (0, 2), pipeline_mode=pl.Buffered(1)),
                pl.BlockSpec((BQ, width), lambda i, s: (i, 0)),
                pl.BlockSpec((16, BQ), lambda i, s: (0, i)),
                pl.BlockSpec((total // BK, 1, BK), lambda i, s: (0, 0, 0)),
            ],
            out_specs=pl.BlockSpec((BQ, width), lambda i, s: (i, 0)),
            scratch_shapes=[pltpu.VMEM((total // BK, BK, BQ), F32)],
        ),
        out_shape=jax.ShapeDtypeStruct((rows, width), BF16),
        compiler_params=pltpu.CompilerParams(
            dimension_semantics=("arbitrary",), vmem_limit_bytes=LIMIT
        ),
        cost_estimate=COST,
        name="query_grads",
    )(scalars, qkv, qkv, qkv, dout, stats, kb)


def key_kernel(s_ref, k_ref, v_ref, q_ref, do_ref, stat_ref, mask_ref, dk_ref, dv_ref, *, pair, per):
    total = q_ref.shape[0]
    b1, b2 = s_ref[0], s_ref[1]
    first = s_ref[2] + pl.program_id(0) * BK
    lo, hi = key_range(first, first + BK - 1, b1, b2, total)
    j0, j1 = lo // BQ, (hi + BQ - 1) // BQ
    rows = first + lax.broadcasted_iota(jnp.int32, (BK, 1), 0)
    row_seg = segment_of(rows, b1, b2)
    masked = column(mask_ref[0])

    def body(j, carry):
        dk, dv = carry
        span = pl.ds(pl.multiple_of(j * BQ, BQ), BQ)
        cols = j * BQ + lax.broadcasted_iota(jnp.int32, (1, BQ), 1)
        col_seg = segment_of(cols, b1, b2)
        bias = jnp.where(row_seg == col_seg, jnp.where(rows == cols, 0.0, masked), NEG)
        queries, grads = q_ref[span, :], do_ref[span, :]
        place = ((j // per) ^ s_ref[3]) * per + lax.rem(j, per)
        spot = pl.ds(pl.multiple_of(place * BQ, BQ), BQ)
        for side in range(2):
            h = 2 * pair + side
            qh, gh = pick(queries, side), pick(grads, side)
            prob = jnp.exp2(dot(k_ref[...], qh, ROW) + bias - stat_ref[h : h + 1, spot])
            score = prob * (dot(v_ref[...], gh, ROW) - stat_ref[8 + h : 9 + h, spot])
            dk = dk + dot(score.astype(BF16), qh)
            dv = dv + dot(prob.astype(BF16), gh)
        return dk, dv

    zero = jnp.zeros((BK, 128), F32)
    dk, dv = lax.fori_loop(j0, j1, body, (zero, zero))
    dk_ref[...] = (dk * (1.0 / LOG2E)).astype(BF16)
    dv_ref[...] = dv.astype(BF16)


def key_grads(scalars, qkv, dout, stats, kb, rows, pairs, pair):
    total = qkv.shape[0]

    def kernel(*refs):
        key_kernel(*refs, pair=pair, per=rows // BQ)

    return pl.pallas_call(
        kernel,
        grid_spec=pltpu.PrefetchScalarGridSpec(
            num_scalar_prefetch=1,
            grid=(rows // BK,),
            in_specs=[
                pl.BlockSpec((BK, 128), lambda i, s: (s[2] // BK + i, pairs + pair)),
                pl.BlockSpec((BK, 128), lambda i, s: (s[2] // BK + i, 2 * pairs + pair)),
                pl.BlockSpec((total, 128), lambda i, s: (0, pair), pipeline_mode=pl.Buffered(1)),
                pl.BlockSpec((total, 128), lambda i, s: (0, pair), pipeline_mode=pl.Buffered(1)),
                pl.BlockSpec((16, total), lambda i, s: (0, 0), pipeline_mode=pl.Buffered(1)),
                pl.BlockSpec((1, 1, BK), lambda i, s: (s[2] // BK + i, 0, 0)),
            ],
            out_specs=[
                pl.BlockSpec((BK, 128), lambda i, s: (i, 0)),
                pl.BlockSpec((BK, 128), lambda i, s: (i, 0)),
            ],
        ),
        out_shape=[jax.ShapeDtypeStruct((rows, 128), BF16)] * 2,
        compiler_params=pltpu.CompilerParams(
            dimension_semantics=("arbitrary",), vmem_limit_bytes=LIMIT
        ),
        cost_estimate=PAIR_COST,
        name="key_grads",
    )(scalars, qkv, qkv, qkv, dout, stats, kb)


def put(out_ref, piece, height, start, low=0):
    unit = 192 if height % 192 == 0 else 16
    span = pl.ds(pl.multiple_of(start, unit), height)
    if len(piece.shape) == 3:
        wide = piece.shape[2]
        for k in range(piece.shape[0]):
            out_ref[span, k * wide : (k + 1) * wide] = piece[k]
    else:
        wide = out_ref.shape[1]
        out_ref[span, :] = piece[:height, low : low + wide]


def whole_spec(value):
    zeros = (0,) * value.ndim
    return pl.BlockSpec(value.shape, lambda i, s: zeros, pipeline_mode=pl.Buffered(1))


def place(scalars, pieces, spots, total, cuts):
    count = len(pieces)

    def kernel(s_ref, *refs):
        for i in range(count):
            height, start = spots[i](s_ref)
            for k, (low, wide) in enumerate(cuts):
                put(refs[count + k], refs[i], height, start, low)

    return pl.pallas_call(
        kernel,
        grid_spec=pltpu.PrefetchScalarGridSpec(
            num_scalar_prefetch=1,
            grid=(1,),
            in_specs=[whole_spec(piece) for piece in pieces],
            out_specs=[pl.BlockSpec((total, wide), lambda i, s: (0, 0)) for _, wide in cuts],
        ),
        out_shape=[jax.ShapeDtypeStruct((total, wide), BF16) for _, wide in cuts],
        compiler_params=pltpu.CompilerParams(vmem_limit_bytes=LIMIT),
        name="place",
    )(scalars, *pieces)


def project(scalars, pieces, spots, total, weights, wspots, bias=None, scale=None):
    count, wcount = len(pieces), len(weights)
    depth = pieces[0].shape[1]
    last = weights[0]
    cols = last.shape[1] if last.ndim == 2 else last.shape[0] * last.shape[2]
    block = 512
    extra = [] if bias is None else [bias, scale]
    keep = bias is not None

    def kernel(s_ref, *refs):
        ins, ws = refs[:count], refs[count : count + wcount]
        rest = refs[count + wcount :]
        if keep:
            bias_ref, scale_ref, out_ref, w_ref, x_ref = rest
        else:
            out_ref, x_ref = rest
            w_ref = ws[0]
        step = pl.program_id(0)

        @pl.when(step == 0)
        def _():
            for i in range(count):
                height, start = spots[i](s_ref)
                put(x_ref, ins[i], height, start)
            if keep:
                for i in range(wcount):
                    height, start = wspots[i](s_ref)
                    put(w_ref, ws[i], height, start)

        span = pl.ds(pl.multiple_of(step * block, block), block)
        value = dot(x_ref[span, :], w_ref[...])
        if keep:
            value = (value + bias_ref[...]) * scale_ref[...]
        out_ref[...] = value.astype(BF16)

    out_specs = [pl.BlockSpec((block, cols), lambda i, s: (i, 0))]
    out_shape = [jax.ShapeDtypeStruct((total, cols), BF16)]
    if keep:
        out_specs.append(pl.BlockSpec((depth, cols), lambda i, s: (0, 0)))
        out_shape.append(jax.ShapeDtypeStruct((depth, cols), BF16))
    return pl.pallas_call(
        kernel,
        grid_spec=pltpu.PrefetchScalarGridSpec(
            num_scalar_prefetch=1,
            grid=(total // block,),
            in_specs=[whole_spec(piece) for piece in pieces + weights + extra],
            out_specs=out_specs,
            scratch_shapes=[pltpu.VMEM((total, depth), BF16)],
        ),
        out_shape=out_shape,
        compiler_params=pltpu.CompilerParams(
            dimension_semantics=("arbitrary",), vmem_limit_bytes=LIMIT
        ),
        cost_estimate=pl.CostEstimate(
            flops=2 * total * depth * cols, transcendentals=0, bytes_accessed=4_000_000
        ),
        name="project",
    )(scalars, *pieces, *weights, *extra)


def call_rows(kernel, rows, name, blocked, fixed, outs, kept=(), flops=0):
    specs = [pl.BlockSpec((BQ,) + v.shape[1:], lambda i: (i, 0)) for v in blocked]
    specs += [pl.BlockSpec(v.shape, lambda i: (0, 0), pipeline_mode=pl.Buffered(1)) for v in fixed]
    shapes, out_specs = [], []
    for wide, kind in outs:
        if kind == "turned":
            shapes.append(jax.ShapeDtypeStruct((8, rows), F32))
            out_specs.append(pl.BlockSpec((8, BQ), lambda i: (0, i)))
        else:
            shapes.append(jax.ShapeDtypeStruct((rows, wide), kind))
            out_specs.append(pl.BlockSpec((BQ, wide), lambda i: (i, 0)))
    for wide in kept:
        shapes.append(jax.ShapeDtypeStruct((8, wide), F32))
        out_specs.append(pl.BlockSpec((8, wide), lambda i: (0, 0)))
    return pl.pallas_call(
        kernel,
        grid=(rows // BQ,),
        in_specs=specs,
        out_specs=out_specs,
        out_shape=shapes,
        compiler_params=pltpu.CompilerParams(
            dimension_semantics=("arbitrary",), vmem_limit_bytes=LIMIT
        ),
        cost_estimate=pl.CostEstimate(flops=flops, transcendentals=0, bytes_accessed=4_000_000),
        name=name,
    )(*blocked, *fixed)


def upper_kernel(
    tok, mine, other, gains, shifts, bias, w_up, w_low, normed_ref, factor_ref, low_ref, active_ref, slope_ref, part_ref
):
    total = tok[...].astype(F32) + (mine[...].astype(F32) + other[...].astype(F32)) + shifts[0:1, :]
    normed, factor = normalize(total)
    normed_ref[...] = normed
    factor_ref[...] = jnp.broadcast_to(factor, factor_ref.shape)
    low = (normed * gains[0:1, :] + shifts[1:2, :]).astype(BF16)
    low_ref[...] = low
    acc = jnp.zeros(part_ref.shape, F32)
    step = 512
    for k in range(w_up.shape[1] // step):
        span = slice(k * step, k * step + step)
        upper = dot(low, w_up[:, span]) + bias[:, span]
        half = 0.5 + 0.5 * lax.erf(upper * 0.7071067811865476)
        bell = jnp.exp2(upper * upper * (-0.5 * LOG2E)) * 0.3989422804014327
        slope_ref[:, span] = half + upper * bell
        active = (upper * half).astype(BF16)
        active_ref[:, span] = active
        acc = acc + dot(active, w_low[:, span], ROW)
    part_ref[...] = acc.astype(BF16)


def lower_kernel(
    normed_ref, mine, other, cot, slope, gains, shifts, w_up, w_low, out_ref, grad_ref, low_ref, up_ref, part_ref, sum_ref
):
    first = normed_ref[...] * gains[0:1, :] + shifts[1:2, :]
    total = first + (mine[...].astype(F32) + other[...].astype(F32)) + shifts[2:3, :]
    normed, factor = normalize(total)
    out_ref[...] = (normed * gains[1:2, :] + shifts[3:4, :]).astype(BF16)
    upstream = cot[...].astype(F32)
    grad = norm_back(upstream, normed, factor, gains[1:2, :])
    grad_ref[...] = grad
    low = grad.astype(BF16)
    low_ref[...] = low
    dim = low.shape[1]

    @pl.when(pl.program_id(0) == 0)
    def _():
        sum_ref[...] = jnp.zeros_like(sum_ref)

    sum_ref[0:1, :dim] += jnp.sum(upstream * normed, axis=0, keepdims=True)
    sum_ref[1:2, :dim] += jnp.sum(upstream, axis=0, keepdims=True)
    sum_ref[2:3, :dim] += jnp.sum(grad, axis=0, keepdims=True)
    acc = jnp.zeros(part_ref.shape, F32)
    step = 512
    for k in range(w_up.shape[1] // step):
        span = slice(k * step, k * step + step)
        up = (dot(low, w_low[:, span]) * slope[:, span]).astype(BF16)
        up_ref[:, span] = up
        sum_ref[3:4, span] += jnp.sum(up.astype(F32), axis=0, keepdims=True)
        acc = acc + dot(up, w_up[:, span], ROW)
    part_ref[...] = acc.astype(BF16)


def branch_kernel(
    grad, mine, other, normed_ref, factor, att, gains, sums, w_back, first_ref, low_ref, dout_ref, delta_ref, sum_ref
):
    upstream = grad[...] + (mine[...].astype(F32) + other[...].astype(F32))
    normed = normed_ref[...]
    back = norm_back(upstream, normed, factor[:, :1], gains[0:1, :])
    first_ref[...] = back
    low = back.astype(BF16)
    low_ref[...] = low
    dim = low.shape[1]

    @pl.when(pl.program_id(0) == 0)
    def _():
        sum_ref[...] = sums[...]

    sum_ref[0:1, dim:] += jnp.sum(upstream * normed, axis=0, keepdims=True)
    sum_ref[1:2, dim:] += jnp.sum(upstream, axis=0, keepdims=True)
    sum_ref[2:3, dim:] += jnp.sum(back, axis=0, keepdims=True)
    dout = dot(low, w_back[...]).astype(BF16)
    dout_ref[...] = dout
    delta_ref[...] = jnp.zeros_like(delta_ref)
    for p in range(dout.shape[1] // 128):
        span = slice(p * 128, p * 128 + 128)
        turned = jnp.transpose(dout[:, span].astype(F32) * att[:, span].astype(F32))
        delta_ref[2 * p : 2 * p + 1, :] = jnp.sum(turned[:64], axis=0, keepdims=True)
        delta_ref[2 * p + 1 : 2 * p + 2, :] = jnp.sum(turned[64:], axis=0, keepdims=True)


def split(value):
    high = lax.reduce_precision(value, 8, 7)
    return high.astype(BF16), (value - high).astype(BF16)


def after(value, *others):
    return lax.optimization_barrier((value, others))[0]


def solution(mesh):
    n_fsdp, n_context = mesh.shape["fsdp"], mesh.shape["context"]
    direct_f, direct_c = n_fsdp == 4, n_context == 4
    swap = [(0, 1), (1, 0)]

    def partner(value, axis, d):
        return lax.ppermute(value, axis, [(i, i ^ d) for i in range(4)])

    def twin(value):
        return lax.ppermute(value, "tensor", swap)

    def pair_sum(value):
        low = value.astype(BF16)
        return low.astype(F32) + twin(low).astype(F32)

    def send_weight(shard, axis=0):
        if not direct_f:
            return [lax.all_gather(shard, "fsdp", axis=axis, tiled=True)]
        return [shard] + [partner(shard, "fsdp", d) for d in (1, 2, 3)]

    def weight_spots(pieces, axis=0):
        rows = pieces[0].shape[axis]
        if not direct_f:
            return [lambda s: (rows, 0)]
        return [lambda s, d=d: (rows, (s[6] ^ d) * rows) for d in range(4)]

    def send_rows(block, stats=None):
        if not direct_c:
            whole = lax.all_gather(block, "context", axis=0, tiled=True)
            if stats is None:
                return [whole]
            return [whole, lax.all_gather(stats, "context", axis=1, tiled=True)]
        half = block.shape[0] // 2
        mine = lax.dynamic_slice_in_dim(block, lax.axis_index("tensor") * half, half, 0)
        if stats is not None:
            mine = jnp.concatenate((mine,) + split(stats), axis=0)
        near = partner(mine, "context", 1)
        far = partner(mine, "context", 2)
        inner = lax.ppermute(mine, "context", [(1, 2), (2, 1)])
        return [near, far, inner]

    def row_pieces(block, got):
        if not direct_c:
            rows = got[0].shape[0]
            return got[:1], [lambda s: (rows, 0)]
        rows = block.shape[0]
        half = rows // 2
        pieces, spots = [block], [lambda s: (rows, s[4] * rows)]
        for d in (1, 2, 3):
            pieces.append(got[d - 1])
            spots.append(lambda s, d=d: (half, (s[4] ^ d) * rows + s[5] * half))
            pieces.append(twin(got[d - 1]))
            spots.append(lambda s, d=d: (half, (s[4] ^ d) * rows + (1 - s[5]) * half))
        return pieces, spots

    def row_stats(stats, got, half):
        if not direct_c:
            return got[1]
        both = [piece[half : half + 16].astype(F32) + piece[half + 16 :].astype(F32) for piece in got]
        return jnp.concatenate([stats] + both, axis=1)

    def pack(small, cols):
        high, low = split(small)
        filler = jnp.zeros((16 - 2 * small.shape[0], cols), BF16)
        return jnp.concatenate([high, low, filler], axis=0)

    def unpack(block, rows):
        return block[:rows].astype(F32) + block[rows : 2 * rows].astype(F32)

    def send_f(partials, small=None):
        if not direct_f:
            whole = jnp.concatenate(partials, axis=1)
            share = lax.psum_scatter(whole, "fsdp", scatter_dimension=0, tiled=True)
            return [share], None if small is None else lax.psum(small, "fsdp")
        me, rows = lax.axis_index("fsdp"), partials[0].shape[0] // 4
        cols = sum([partial.shape[1] for partial in partials])
        extra = [] if small is None else [pack(small, cols)]
        blocks = []
        for d in range(4):
            cut = [lax.dynamic_slice_in_dim(p, (me ^ d) * rows, rows, 0) for p in partials]
            piece = jnp.concatenate(cut, axis=1) if len(cut) > 1 else cut[0]
            if d:
                piece = jnp.concatenate([piece] + extra, axis=0) if extra else piece
                piece = partner(piece, "fsdp", d)
            blocks.append(piece)
        return blocks, small

    def finish_f(blocks, small=None):
        if not direct_f:
            return blocks[0], small
        rows = blocks[0].shape[0]
        parts = [block[:rows].astype(F32) for block in blocks]
        share = ((parts[0] + parts[1]) + (parts[2] + parts[3])).astype(BF16)
        if small is None:
            return share, None
        more = [unpack(block[rows:], small.shape[0]) for block in blocks[1:]]
        return share, (small + more[0]) + (more[1] + more[2])

    def send_z(mine, theirs, small, d):
        if small is not None:
            theirs = jnp.concatenate([theirs, pack(small, mine.shape[1])], axis=0)
        return (mine, partner(theirs, "context", d), small)

    def send_1(share, small=None):
        if not direct_c:
            return (share, small)
        side, rows = lax.rem(lax.axis_index("context"), 2), share.shape[0] // 2
        mine = lax.dynamic_slice_in_dim(share, side * rows, rows, 0)
        theirs = lax.dynamic_slice_in_dim(share, (1 - side) * rows, rows, 0)
        return send_z(mine, theirs, small, 1)

    def finish_z(state):
        if not direct_c:
            return state
        mine, got, small = state
        rows = mine.shape[0]
        total = (mine.astype(F32) + got[:rows].astype(F32)).astype(BF16)
        if small is not None:
            small = small + unpack(got[rows:], small.shape[0])
        return total, small

    def send_2(share, small=None):
        if not direct_c:
            return (share, small)
        return send_z(share, share, small, 2)

    def send_3(share, small=None):
        if not direct_c:
            total = lax.psum(share, "context")
            return (total, None if small is None else lax.psum(small, "context"))
        return (share, partner(share, "context", 1), small)

    def finish_3(state):
        if not direct_c:
            return state[0].astype(F32), state[1]
        share, other, small = state
        side = lax.rem(lax.axis_index("context"), 2)
        first = jnp.where(side == 0, share, other)
        second = jnp.where(side == 0, other, share)
        return jnp.concatenate([first, second], axis=0).astype(F32), small

    def shards(
        tokens,
        cotangent,
        w_qkv,
        bias_qv,
        w_attn_out,
        w_up,
        bias_up,
        w_down,
        gains,
        shifts,
        seq_lengths,
        key_mask,
    ):
        rows = tokens.shape[0]
        width = w_qkv.shape[2]
        pairs = width // 128
        hidden = w_up.shape[1]
        total = key_mask.shape[0]
        dim = tokens.shape[1]
        b1 = seq_lengths[0, 0]
        b2 = b1 + seq_lengths[0, 1]
        me = lax.axis_index("context")
        order = me if direct_c else 0 * me
        scalars = jnp.stack(
            [b1, b2, me * rows, order, me, lax.axis_index("tensor"), lax.axis_index("fsdp")]
        ).astype(jnp.int32)
        kb = jnp.where(key_mask == 1, 0.0, NEG).astype(F32).reshape(total // BK, 1, BK)

        got = send_rows(tokens)
        wq = send_weight(w_qkv, 1)
        got, wq = lax.optimization_barrier((got, wq))
        shard = jnp.concatenate([w_attn_out.T, w_up, w_down.T], axis=1)
        rest = send_weight(after(shard, wq[-1]))
        cuts = [(0, width), (width, hidden), (width + hidden, hidden)]
        zero = jnp.zeros((width,), F32)
        bias_row = jnp.concatenate([bias_qv[0], zero, bias_qv[1]]).reshape(1, -1)
        scale_row = jnp.concatenate([zero + 0.125 * LOG2E, zero + 1.0, zero + 1.0]).reshape(1, -1)
        pieces, spots = row_pieces(tokens, got)
        qkv, w_proj = project(
            scalars, pieces, spots, total, wq, weight_spots(wq, 1), bias_row, scale_row
        )
        attended, lset = attend(scalars, qkv, kb, rows, pairs)
        rest = after(rest, attended)
        w_back, w_upper, w_lower = place(scalars, rest, weight_spots(rest), dim, cuts)

        part = dot(attended, w_back, ROW).astype(BF16)
        work = 4 * rows * dim * hidden
        normed1, factor1, first_low, active, slope, part = call_rows(
            upper_kernel,
            rows,
            "upper",
            [tokens, part, twin(part)],
            [gains, shifts, bias_up.reshape(1, hidden), w_upper, w_lower],
            [(dim, F32), (128, F32), (dim, BF16), (hidden, BF16), (hidden, F32), (dim, BF16)],
            flops=2 * work,
        )
        out, grad_second, lower_grad, grad_upper, part, sums = call_rows(
            lower_kernel,
            rows,
            "lower",
            [normed1, part, twin(part), cotangent, slope],
            [gains, shifts, w_upper, w_lower],
            [(dim, BF16), (dim, F32), (dim, BF16), (hidden, BF16), (dim, BF16)],
            [hidden],
            flops=work,
        )
        other = twin(part)
        group_a, _ = send_f([dot(lower_grad.T, active).astype(BF16)])
        grad_first_sum, branch_grad, dout, deltat, small = call_rows(
            branch_kernel,
            rows,
            "branch",
            [grad_second, part, other, normed1, factor1, attended],
            [gains, sums, w_back],
            [(dim, F32), (dim, BF16), (width, BF16), (8, "turned")],
            [hidden],
            flops=work // 8,
        )
        stats = jnp.concatenate([lset, deltat], axis=0)
        got = send_rows(branch_grad, stats)
        group_b, small = send_f([dot(first_low.T, grad_upper).astype(BF16)], small)
        dq = query_grads(scalars, qkv, dout, stats, kb, rows, pairs)

        got = after(got, dq)
        stats_all = row_stats(stats, got, rows // 2)
        pieces, spots = row_pieces(branch_grad, got)
        (dout_all,) = project(scalars, pieces, spots, total, [w_back], None)
        group_a, _ = finish_f(after(group_a, dq))
        group_b, small = finish_f(after(group_b, dq), small)
        state_a, state_b = send_1(group_a), send_1(group_b, small)
        dks, dvs = [], []
        gate = (group_a, group_b)
        for pair in range(pairs):
            dk, dv = key_grads(
                after(scalars, gate), qkv, dout_all, stats_all, kb, rows, pairs, pair
            )
            dks.append(dk)
            dvs.append(dv)
            if pair == 0:
                group_a, group_b = finish_z(after(state_a, dk)), finish_z(after(state_b, dk))
                state_a, state_b = send_2(*group_a), send_2(*group_b)
                gate = (group_a, group_b)
            elif pair == 1:
                group_a, group_b = finish_z(after(state_a, dk)), finish_z(after(state_b, dk))
                state_a, state_b = send_3(*group_a), send_3(*group_b)
                early = jnp.concatenate([dq] + dks + dvs, axis=1)
                sums = jnp.sum(early.astype(F32), axis=0, keepdims=True)
                row = jnp.pad(sums, ((0, 0), (0, width)))
                group_c, row = send_f(
                    [
                        dot(tokens.T, early).astype(BF16),
                        dot(branch_grad.T, attended).astype(BF16),
                    ],
                    row,
                )
                gate = (group_a, group_b)
        late = jnp.concatenate([dks[-1], dvs[-1]], axis=1)
        tail = jnp.sum(late.astype(F32), axis=0, keepdims=True)
        group_d, tail = send_f([dot(tokens.T, late).astype(BF16)], tail)
        group_c, row = finish_f(after(group_c, late), row)
        state_c = send_1(group_c, row)
        stacked = jnp.concatenate([dq] + dks + dvs, axis=1)
        input_part = pair_sum(dot(stacked, w_proj, ROW))
        grad_tokens = (grad_first_sum + input_part).astype(BF16)
        group_d, tail = finish_f(group_d, tail)
        state_d = send_1(group_d, tail)
        state_c, state_d = send_2(*finish_z(state_c)), send_2(*finish_z(state_d))
        group_a, _ = finish_3(after(state_a, late))
        group_b, small = finish_3(after(state_b, late))
        state_c, state_d = send_3(*finish_z(state_c)), send_3(*finish_z(state_d))
        group_c, row = finish_3(state_c)
        group_d, tail = finish_3(state_d)

        sum_gains = jnp.stack([small[0, dim:], small[0, :dim]])
        sum_shifts = jnp.stack([small[2, dim:], small[1, dim:], small[2, :dim], small[1, :dim]])
        sum_bias_up = small[3]
        near_k = width + width - 128
        near_v = near_k + width - 128
        sum_bias_qv = jnp.stack(
            [row[0, :width], jnp.concatenate([row[0, near_k:near_v], tail[0, 128:]])]
        )
        share_qkv = jnp.stack(
            [
                group_c[:, :width],
                jnp.concatenate([group_c[:, width:near_k], group_d[:, :128]], axis=1),
                jnp.concatenate([group_c[:, near_k:near_v], group_d[:, 128:]], axis=1),
            ]
        )
        share_lower = group_a.T
        share_upper = group_b
        share_back = group_c[:, near_v:].T
        return (
            out,
            grad_tokens,
            share_qkv,
            share_back,
            share_upper,
            share_lower,
            sum_bias_qv,
            sum_bias_up,
            sum_gains,
            sum_shifts,
        )

    return jax.shard_map(
        shards,
        mesh=mesh,
        in_specs=(
            P(("fsdp", "context"), None),
            P(("fsdp", "context"), None),
            P(None, "fsdp", "tensor"),
            P(None, "tensor"),
            P("tensor", "fsdp"),
            P("fsdp", "tensor"),
            P("tensor"),
            P("tensor", "fsdp"),
            P(),
            P(),
            P("fsdp", None),
            P("fsdp"),
        ),
        out_specs=(
            P(("fsdp", "context"), None),
            P(("fsdp", "context"), None),
            P(None, "fsdp", "tensor"),
            P("tensor", "fsdp"),
            P("fsdp", "tensor"),
            P("tensor", "fsdp"),
            P(None, "tensor"),
            P("tensor"),
            P(),
            P(),
        ),
        check_vma=False,
    )
```

profile of v0, /device:TPU:0, one launch (start us, length us, event | category | flops | bytes accessed | tf_op | source)
XLA Modules:
  0.0 407.1 jit_solution(9029507852687700364)
XLA Ops:
  0.7 3.0 collective-permute-start.3
  3.7 1.1 constant_dynamic-slice_fusion.19
  4.8 1.6 collective-permute-start
  6.4 2.6 collective-permute-start.1
  9.0 1.5 collective-permute-start.2
  10.5 1.5 collective-permute-start.4
  12.1 2.0 collective-permute-done.3.refs_8_
  14.1 2.7 collective-permute-start.5
  18.2 1.3 compare_select_fusion
  19.5 11.9 %collective-permute-done.4.refs_9_ = bf16[3,192,384]{2,1,0:T(8,128)(2,1)} collective-permute-done((bf16[3,192,384]{2,1,0:T(8,128)(2,1)}, bf16[3,192,384]{2,1,0:T(8,128)(2,1)}, u32[]{:S(2)}, u32[]{:S(2)}) %collective-permute-start.4) | collective-permute-done | bytes 442400 | tf_op jit(solution)/shard_map/ppermute | solution.py:523
  31.4 4.8 %collective-permute-done.1.refs_3_ = bf16[384,768]{1,0:T(8,128)(2,1)S(1)} collective-permute-done((bf16[384,768]{1,0:T(8,128)(2,1)S(1)}, bf16[384,768]{1,0:T(8,128)(2,1)S(1)}, u32[]{:S(2)}, u32[]{:S(2)}) %collective-permute-start.1) | collective-permute-done | bytes 589856 | tf_op jit(solution)/shard_map/ppermute | solution.py:523
  36.8 1.3 fusion.32
  39.5 1.2 stack.48.s_ref.refs_0_
  41.8 1.6 collective-permute-start.10
  43.8 1.5 collective-permute-start.9
  45.3 12.5 %project.2 = (bf16[3072,1152]{1,0:T(8,128)(2,1)}, bf16[768,1152]{1,0:T(8,128)(2,1)}) custom-call(s32[7]{0:T(128)} %stack.48.s_ref.refs_0_, bf16[768,768]{1,0:T(8,128)(2,1)} %tok.1, bf16[384,768]{1,0:T(8,128)(2,1)} %copy-done.43, bf16[384,768]{1,0:T(8,128)(2,1)} %copy-done.45, bf16[384,768]{1,0:T(8,128)(2,1)} %copy-done.44, ...), custom_call_target="tpu_custom_call" | custom-call | flops 5435817984 | bytes 4000000 | tf_op jit(solution)/shard_map/project/pallas_call | solution.py:377
  57.9 29.5 %attend.1 = (bf16[768,384]{1,0:T(8,128)(2,1)}, f32[8,768]{1,0:T(8,128)}) custom-call(s32[7]{0:T(128)} %stack.48.s_ref.refs_0_, bf16[3072,1152]{1,0:T(8,128)(2,1)} %get-tuple-element.92.q_ref.k_ref.v_ref.refs_1_.refs_2_.refs_3_, bf16[3072,1152]{1,0:T(8,128)(2,1)} %get-tuple-element.92.q_ref.k_ref.v_ref.refs_1_.refs_2_.refs_3_, ...), custom_call_target="tpu_custom_call" | custom-call | flops 35999997952 | bytes 8000000 | tf_op jit(solution)/shard_map/attend/pallas_call | solution.py:130
  87.4 14.3 %collective-permute-done.10.refs_2_ = bf16[192,3456]{1,0:T(8,128)(2,1)S(1)} collective-permute-done((bf16[192,3456]{1,0:T(8,128)(2,1)S(1)}, bf16[192,3456]{1,0:T(8,128)(2,1)S(1)}, u32[]{:S(2)}, u32[]{:S(2)}) %collective-permute-start.10) | collective-permute-done | bytes 1327136 | tf_op jit(solution)/shard_map/ppermute | solution.py:523
  101.7 1.2 collective-permute-done.9.refs_1_
  104.0 5.9 %place.1 = (bf16[768,384]{1,0:T(8,128)(2,1)}, bf16[768,1536]{1,0:T(8,128)(2,1)}, bf16[768,1536]{1,0:T(8,128)(2,1)}) custom-call(s32[7]{0:T(128)} %stack.48.s_ref.refs_0_, bf16[192,3456]{1,0:T(8,128)(2,1)} %copy-done, bf16[192,3456]{1,0:T(8,128)(2,1)} %copy-done.8, bf16[192,3456]{1,0:T(8,128)(2,1)} %copy-done.6, bf16[192,3456]{1,0:T(8,128)(2,1)} %copy-done.7), custom_call_target="tpu_custom_call" | custom-call | tf_op jit(solution)/shard_map/place/pallas_call | solution.py:323
  110.0 1.9 convolution_convert_fusion.4.mine
  112.7 2.1 collective-permute-done.12.other
  115.8 10.9 %upper.1 = (f32[768,768]{1,0:T(8,128)}, f32[768,128]{1,0:T(8,128)}, bf16[768,768]{1,0:T(8,128)(2,1)}, bf16[768,1536]{1,0:T(8,128)(2,1)}, f32[768,1536]{1,0:T(8,128)}, /*index=5*/bf16[768,768]{1,0:T(8,128)(2,1)}) custom-call(bf16[768,768]{1,0:T(8,128)(2,1)} %tok.1, bf16[768,768]{1,0:T(8,128)(2,1)} %copy-done.11, bf16[768,768]{1,0:T(8,128)(2,1)} %copy-done.42, ...), custom_call_target="tpu_custom_call" | custom-call | flops 7247757312 | bytes 4000000 | tf_op jit(solution)/shard_map/upper/pallas_call | solution.py:411
  126.9 2.9 collective-permute-done.13.other
  130.8 12.3 %lower.1 = (bf16[768,768]{1,0:T(8,128)(2,1)}, f32[768,768]{1,0:T(8,128)}, bf16[768,768]{1,0:T(8,128)(2,1)}, bf16[768,1536]{1,0:T(8,128)(2,1)}, bf16[768,768]{1,0:T(8,128)(2,1)}, /*index=5*/f32[8,1536]{1,0:T(8,128)}) custom-call(f32[768,768]{1,0:T(8,128)} %get-tuple-element.102.normed_ref, bf16[768,768]{1,0:T(8,128)(2,1)} %get-tuple-element.103.mine, ...), custom_call_target="tpu_custom_call" | custom-call | flops 3623878656 | bytes 4000000 | tf_op jit(solution)/shard_map/lower/pallas_call | solution.py:411
  143.3 3.3 convolution_convert_fusion.1
  148.2 1.5 collective-permute-start.16
  149.7 1.4 collective-permute-start.17
  151.1 2.0 convolution_convert_fusion
  154.4 7.7 %branch.1 = (f32[768,768]{1,0:T(8,128)}, bf16[768,768]{1,0:T(8,128)(2,1)}, bf16[768,384]{1,0:T(8,128)(2,1)}, f32[8,768]{1,0:T(8,128)}, f32[8,1536]{1,0:T(8,128)}) custom-call(f32[768,768]{1,0:T(8,128)} %get-tuple-element.106.grad, bf16[768,768]{1,0:T(8,128)(2,1)} %get-tuple-element.107.mine, bf16[768,768]{1,0:T(8,128)(2,1)} %copy-done.10, ...), custom_call_target="tpu_custom_call" | custom-call | flops 452984832 | bytes 4000000 | tf_op jit(solution)/shard_map/branch/pallas_call | solution.py:411
  162.8 1.1 constant_dynamic-slice_fusion.10
  164.0 11.7 %collective-permute-start.21 = (bf16[416,768]{1,0:T(8,128)(2,1)S(1)}, bf16[416,768]{1,0:T(8,128)(2,1)S(1)}, u32[]{:S(2)}, u32[]{:S(2)}) collective-permute-start(bf16[416,768]{1,0:T(8,128)(2,1)S(1)} %pad_maximum_fusion.17), channel_id=1, source_target_pairs={{0,2},{2,0},{4,6},{6,4},{1,3},{3,1},{5,7},{7,5},{8,10},{10,8},{12,... | collective-permute-start | bytes 1916936 | tf_op jit(solution)/shard_map/ppermute | solution.py:523
  176.8 1.3 pad_maximum_fusion.1
  179.4 1.5 collective-permute-start.19
  180.9 21.6 %collective-permute-done.21.refs_1_ = bf16[416,768]{1,0:T(8,128)(2,1)S(1)} collective-permute-done((bf16[416,768]{1,0:T(8,128)(2,1)S(1)}, bf16[416,768]{1,0:T(8,128)(2,1)S(1)}, u32[]{:S(2)}, u32[]{:S(2)}) %collective-permute-start.21) | collective-permute-done | bytes 639008 | tf_op jit(solution)/shard_map/ppermute | solution.py:523
  202.5 1.6 collective-permute-start.20
  204.1 46.9 %query_grads.1 = bf16[768,384]{1,0:T(8,128)(2,1)} custom-call(s32[7]{0:T(128)} %stack.48.s_ref.refs_0_, bf16[3072,1152]{1,0:T(8,128)(2,1)} %get-tuple-element.92.q_ref.k_ref.v_ref.refs_1_.refs_2_.refs_3_, bf16[3072,1152]{1,0:T(8,128)(2,1)} %get-tuple-element.92.q_ref.k_ref.v_ref.refs_1_.refs_2_.refs_3_, ...), custom_call_target="tpu_custom_call" | custom-call | flops 35999997952 | bytes 8000000 | tf_op jit(solution)/shard_map/query_grads/pallas_call | solution.py:205
  255.6 2.0 add_convert_fusion.1
  257.9 2.0 collective-permute-start.27
  262.5 8.2 %project.3.refs_4_ = bf16[3072,384]{1,0:T(8,128)(2,1)} custom-call(s32[7]{0:T(128)} %stack.48.s_ref.refs_0_, bf16[768,768]{1,0:T(8,128)(2,1)} %get-tuple-element.128.refs_0_, bf16[416,768]{1,0:T(8,128)(2,1)} %copy-done.12, bf16[416,768]{1,0:T(8,128)(2,1)} %copy-done.15, bf16[416,768]{1,0:T(8,128)(2,1)} %copy-done.13, bf16[416,768]{1,0:T(8,128)(2,1)} %copy-done.16, ...), custom_call_target="tpu_custom_call" | custom-call | flops 1811939328 | bytes 4000000 | tf_op jit(solution)/shard_map/project/pallas_call | solution.py:377
  270.7 16.3 %key_grads.3 = (bf16[768,128]{1,0:T(8,128)(2,1)}, bf16[768,128]{1,0:T(8,128)(2,1)}) custom-call(s32[7]{0:T(128)} %stack.48.s_ref.refs_0_, bf16[3072,1152]{1,0:T(8,128)(2,1)} %get-tuple-element.92.q_ref.k_ref.v_ref.refs_1_.refs_2_.refs_3_, bf16[3072,1152]{1,0:T(8,128)(2,1)} %get-tuple-element.92.q_ref.k_ref.v_ref.refs_1_.refs_2_.refs_3_, ...), custom_call_target="tpu_custom_call" | custom-call | flops 14000000000 | bytes 4000000 | tf_op jit(solution)/shard_map/key_grads/pallas_call | solution.py:270
  287.3 7.8 %collective-permute-start.29 = (bf16[96,1536]{1,0:T(8,128)(2,1)S(1)}, bf16[96,1536]{1,0:T(8,128)(2,1)S(1)}, u32[]{:S(2)}, u32[]{:S(2)}) collective-permute-start(bf16[96,1536]{1,0:T(8,128)(2,1)S(1)} %add_convert_fusion.7), channel_id=1, source_target_pairs={{0,4},{2,6},{4,0},{6,2},{1,5},{3,7},{5,1},{7,3},{8,12},{10,14},{12... | collective-permute-start | bytes 884744 | tf_op jit(solution)/shard_map/ppermute | solution.py:523
  295.1 16.3 %key_grads.4 = (bf16[768,128]{1,0:T(8,128)(2,1)}, bf16[768,128]{1,0:T(8,128)(2,1)}) custom-call(s32[7]{0:T(128)} %stack.48.s_ref.refs_0_, bf16[3072,1152]{1,0:T(8,128)(2,1)} %get-tuple-element.92.q_ref.k_ref.v_ref.refs_1_.refs_2_.refs_3_, bf16[3072,1152]{1,0:T(8,128)(2,1)} %get-tuple-element.92.q_ref.k_ref.v_ref.refs_1_.refs_2_.refs_3_, ...), custom_call_target="tpu_custom_call" | custom-call | flops 14000000000 | bytes 4000000 | tf_op jit(solution)/shard_map/key_grads/pallas_call | solution.py:270
  311.4 2.1 collective-permute-start.30
  313.9 11.7 %collective-permute-done.30 = bf16[112,1536]{1,0:T(8,128)(2,1)S(1)} collective-permute-done((bf16[112,1536]{1,0:T(8,128)(2,1)S(1)}, bf16[112,1536]{1,0:T(8,128)(2,1)S(1)}, u32[]{:S(2)}, u32[]{:S(2)}) %collective-permute-start.30) | collective-permute-done | bytes 344096 | tf_op jit(solution)/shard_map/ppermute | solution.py:523
  325.7 16.5 %key_grads.5 = (bf16[768,128]{1,0:T(8,128)(2,1)}, bf16[768,128]{1,0:T(8,128)(2,1)}) custom-call(s32[7]{0:T(128)} %stack.48.s_ref.refs_0_, bf16[3072,1152]{1,0:T(8,128)(2,1)} %get-tuple-element.92.q_ref.k_ref.v_ref.refs_1_.refs_2_.refs_3_, bf16[3072,1152]{1,0:T(8,128)(2,1)} %get-tuple-element.92.q_ref.k_ref.v_ref.refs_1_.refs_2_.refs_3_, ...), custom_call_target="tpu_custom_call" | custom-call | flops 14000000000 | bytes 4000000 | tf_op jit(solution)/shard_map/key_grads/pallas_call | solution.py:270
  342.2 1.1 constant_dynamic-update-slice_fusion.15
  343.5 1.5 convolution_convert_fusion.2
  347.2 3.4 collective-permute-start.40
  350.7 2.2 collective-permute-done.38
  352.9 1.4 collective-permute-done.39
  354.4 2.2 collective-permute-start.41
  356.6 1.7 convolution_convert_fusion.3
  358.9 2.9 collective-permute-start.42
  361.9 2.2 collective-permute-done.42
  364.0 3.0 collective-permute-start.34
  367.0 2.2 collective-permute-start.43
  369.3 1.1 convert_bitcast_fusion
  371.5 6.3 %collective-permute-done.33 = bf16[208,1280]{1,0:T(8,128)(2,1)S(1)} collective-permute-done((bf16[208,1280]{1,0:T(8,128)(2,1)S(1)}, bf16[208,1280]{1,0:T(8,128)(2,1)S(1)}, u32[]{:S(2)}, u32[]{:S(2)}) %collective-permute-start.33) | collective-permute-done | bytes 532512 | tf_op jit(solution)/shard_map/ppermute | solution.py:523
  379.3 1.1 maximum_convert_fusion
  380.5 7.5 %collective-permute-done.35 = bf16[112,1280]{1,0:T(8,128)(2,1)S(1)} collective-permute-done((bf16[112,1280]{1,0:T(8,128)(2,1)S(1)}, bf16[112,1280]{1,0:T(8,128)(2,1)S(1)}, u32[]{:S(2)}, u32[]{:S(2)}) %collective-permute-start.35) | collective-permute-done | bytes 286752 | tf_op jit(solution)/shard_map/ppermute | solution.py:523
  390.1 8.8 %collective-permute-done.36 = bf16[112,1280]{1,0:T(8,128)(2,1)S(1)} collective-permute-done((bf16[112,1280]{1,0:T(8,128)(2,1)S(1)}, bf16[112,1280]{1,0:T(8,128)(2,1)S(1)}, u32[]{:S(2)}, u32[]{:S(2)}) %collective-permute-start.36) | collective-permute-done | bytes 286752 | tf_op jit(solution)/shard_map/ppermute | solution.py:523
  399.6 1.4 add_convert_fusion
  401.0 4.2 %collective-permute-done.37 = bf16[96,1280]{1,0:T(8,128)(2,1)S(1)} collective-permute-done((bf16[96,1280]{1,0:T(8,128)(2,1)S(1)}, bf16[96,1280]{1,0:T(8,128)(2,1)S(1)}, u32[]{:S(2)}, u32[]{:S(2)}) %collective-permute-start.37) | collective-permute-done | bytes 245792 | tf_op jit(solution)/shard_map/ppermute | solution.py:523
  (252 shorter events, 32.2 us)
Async XLA Ops:
  0.6 40.1 %copy-start.24 = (bf16[1536,192]{0,1:T(8,128)(2,1)S(1)}, bf16[1536,192]{0,1:T(8,128)(2,1)}, u32[]{:S(2)}) copy-start(bf16[1536,192]{0,1:T(8,128)(2,1)} %param.19) | copy-start | bytes 1769476
  0.7 40.1 %copy-start.25 = (bf16[192,1536]{1,0:T(8,128)(2,1)S(1)}, bf16[192,1536]{1,0:T(8,128)(2,1)}, u32[]{:S(2)}) copy-start(bf16[192,1536]{1,0:T(8,128)(2,1)} %param.17) | copy-start | bytes 1769476
  0.7 13.4 %collective-permute-start.3 = (bf16[3,192,384]{2,1,0:T(8,128)(2,1)}, bf16[3,192,384]{2,1,0:T(8,128)(2,1)S(1)}, u32[]{:S(2)}, u32[]{:S(2)}) collective-permute-start(bf16[3,192,384]{2,1,0:T(8,128)(2,1)} %refs_7_), channel_id=1, source_target_pairs={{0,8},{8,0},{16,24},{24,16},{1,9},{9,1},{17,25},{25,17},{2,10},{10... | collective-permute-start | bytes 1327112 | tf_op jit(solution)/shard_map/ppermute | solution.py:523
  4.8 26.6 %collective-permute-start = (bf16[384,768]{1,0:T(8,128)(2,1)S(1)}, bf16[384,768]{1,0:T(8,128)(2,1)S(1)}, u32[]{:S(2)}, u32[]{:S(2)}) collective-permute-start(bf16[384,768]{1,0:T(8,128)(2,1)S(1)} %constant_dynamic-slice_fusion.19), channel_id=1, source_target_pairs={{0,2},{2,0},{4,6},{6,4},{1,3},{3,1},{5,7},{7,5},{8,10},{10,8},{12,... | collective-permute-start | bytes 1769480 | tf_op jit(solution)/shard_map/ppermute | solution.py:523
  6.4 29.7 %collective-permute-start.1 = (bf16[384,768]{1,0:T(8,128)(2,1)S(1)}, bf16[384,768]{1,0:T(8,128)(2,1)S(1)}, u32[]{:S(2)}, u32[]{:S(2)}) collective-permute-start(bf16[384,768]{1,0:T(8,128)(2,1)S(1)} %constant_dynamic-slice_fusion.19), channel_id=1, source_target_pairs={{0,4},{2,6},{4,0},{6,2},{1,5},{3,7},{5,1},{7,3},{8,12},{10,14},{12... | collective-permute-start | bytes 1769480 | tf_op jit(solution)/shard_map/ppermute | solution.py:523
  9.0 27.2 %collective-permute-start.2 = (bf16[384,768]{1,0:T(8,128)(2,1)S(1)}, bf16[384,768]{1,0:T(8,128)(2,1)}, u32[]{:S(2)}, u32[]{:S(2)}) collective-permute-start(bf16[384,768]{1,0:T(8,128)(2,1)S(1)} %constant_dynamic-slice_fusion.19), channel_id=1, source_target_pairs={{2,4},{4,2},{3,5},{5,3},{10,12},{12,10},{11,13},{13,11},{18,20},{2... | collective-permute-start | bytes 1769480 | tf_op jit(solution)/shard_map/ppermute | solution.py:555
  10.5 20.9 %collective-permute-start.4 = (bf16[3,192,384]{2,1,0:T(8,128)(2,1)}, bf16[3,192,384]{2,1,0:T(8,128)(2,1)}, u32[]{:S(2)}, u32[]{:S(2)}) collective-permute-start(bf16[3,192,384]{2,1,0:T(8,128)(2,1)} %refs_7_), channel_id=1, source_target_pairs={{0,16},{8,24},{16,0},{24,8},{1,17},{9,25},{17,1},{25,9},{2,18},{10... | collective-permute-start | bytes 1327112 | tf_op jit(solution)/shard_map/ppermute | solution.py:523
  14.1 27.6 %copy-start.46 = (bf16[3,192,384]{2,1,0:T(8,128)(2,1)}, bf16[3,192,384]{2,1,0:T(8,128)(2,1)S(1)}, u32[]{:S(2)}) copy-start(bf16[3,192,384]{2,1,0:T(8,128)(2,1)S(1)} %collective-permute-done.3.refs_8_) | copy-start | bytes 1327108
  14.1 17.3 %collective-permute-start.5 = (bf16[3,192,384]{2,1,0:T(8,128)(2,1)}, bf16[3,192,384]{2,1,0:T(8,128)(2,1)S(1)}, u32[]{:S(2)}, u32[]{:S(2)}) collective-permute-start(bf16[3,192,384]{2,1,0:T(8,128)(2,1)} %refs_7_), channel_id=1, source_target_pairs={{0,24},{8,16},{16,8},{24,0},{1,25},{9,17},{17,9},{25,1},{2,26},{10... | collective-permute-start | bytes 1327112 | tf_op jit(solution)/shard_map/ppermute | solution.py:523
  31.4 10.3 %copy-start.43 = (bf16[384,768]{1,0:T(8,128)(2,1)}, bf16[384,768]{1,0:T(8,128)(2,1)S(1)}, u32[]{:S(2)}) copy-start(bf16[384,768]{1,0:T(8,128)(2,1)S(1)} %collective-permute-done.refs_1_) | copy-start | bytes 1769476
  36.2 7.6 %collective-permute-start.6 = (bf16[384,768]{1,0:T(8,128)(2,1)S(1)}, bf16[384,768]{1,0:T(8,128)(2,1)S(1)}, u32[]{:S(2)}, u32[]{:S(2)}) collective-permute-start(bf16[384,768]{1,0:T(8,128)(2,1)S(1)} %collective-permute-done.refs_1_), channel_id=1, source_target_pairs={{0,1},{1,0},{2,3},{3,2},{4,5},{5,4},{6,7},{7,6},{8,9},{9,8},{10,11... | collective-permute-start | bytes 1769480 | tf_op jit(solution)/shard_map/ppermute | solution.py:526
  36.3 9.1 %collective-permute-start.7 = (bf16[384,768]{1,0:T(8,128)(2,1)S(1)}, bf16[384,768]{1,0:T(8,128)(2,1)}, u32[]{:S(2)}, u32[]{:S(2)}) collective-permute-start(bf16[384,768]{1,0:T(8,128)(2,1)S(1)} %collective-permute-done.1.refs_3_), channel_id=1, source_target_pairs={{0,1},{1,0},{2,3},{3,2},{4,5},{5,4},{6,7},{7,6},{8,9},{9,8},{10,11... | collective-permute-start | bytes 1769480 | tf_op jit(solution)/shard_map/ppermute | solution.py:526
  36.8 8.6 %collective-permute-start.8 = (bf16[384,768]{1,0:T(8,128)(2,1)}, bf16[384,768]{1,0:T(8,128)(2,1)}, u32[]{:S(2)}, u32[]{:S(2)}) collective-permute-start(bf16[384,768]{1,0:T(8,128)(2,1)} %collective-permute-done.2.refs_5_), channel_id=1, source_target_pairs={{0,1},{1,0},{2,3},{3,2},{4,5},{5,4},{6,7},{7,6},{8,9},{9,8},{10,11... | collective-permute-start | bytes 1769480 | tf_op jit(solution)/shard_map/ppermute | solution.py:526
  41.7 16.1 %copy-start = (bf16[192,3456]{1,0:T(8,128)(2,1)}, bf16[192,3456]{1,0:T(8,128)(2,1)S(1)}, u32[]{:S(2)}) copy-start(bf16[192,3456]{1,0:T(8,128)(2,1)S(1)} %pad_maximum_fusion.refs_0_) | copy-start | bytes 3981316
  41.8 60.0 %collective-permute-start.10 = (bf16[192,3456]{1,0:T(8,128)(2,1)S(1)}, bf16[192,3456]{1,0:T(8,128)(2,1)S(1)}, u32[]{:S(2)}, u32[]{:S(2)}) collective-permute-start(bf16[192,3456]{1,0:T(8,128)(2,1)S(1)} %pad_maximum_fusion.refs_0_), channel_id=1, source_target_pairs={{0,16},{8,24},{16,0},{24,8},{1,17},{9,25},{17,1},{25,9},{2,18},{10... | collective-permute-start | bytes 3981320 | tf_op jit(solution)/shard_map/ppermute | solution.py:523
  43.3 58.4 %collective-permute-start.11 = (bf16[192,3456]{1,0:T(8,128)(2,1)S(1)}, bf16[192,3456]{1,0:T(8,128)(2,1)S(1)}, u32[]{:S(2)}, u32[]{:S(2)}) collective-permute-start(bf16[192,3456]{1,0:T(8,128)(2,1)S(1)} %pad_maximum_fusion.refs_0_), channel_id=1, source_target_pairs={{0,24},{8,16},{16,8},{24,0},{1,25},{9,17},{17,9},{25,1},{2,26},{10... | collective-permute-start | bytes 3981320 | tf_op jit(solution)/shard_map/ppermute | solution.py:523
  43.8 59.1 %collective-permute-start.9 = (bf16[192,3456]{1,0:T(8,128)(2,1)S(1)}, bf16[192,3456]{1,0:T(8,128)(2,1)S(1)}, u32[]{:S(2)}, u32[]{:S(2)}) collective-permute-start(bf16[192,3456]{1,0:T(8,128)(2,1)S(1)} %pad_maximum_fusion.refs_0_), channel_id=1, source_target_pairs={{0,8},{8,0},{16,24},{24,16},{1,9},{9,1},{17,25},{25,17},{2,10},{10... | collective-permute-start | bytes 3981320 | tf_op jit(solution)/shard_map/ppermute | solution.py:523
  111.9 2.9 collective-permute-start.12
  115.8 11.1 %copy-start.39 = (f32[8,768]{1,0:T(8,128)S(1)}, f32[8,768]{1,0:T(8,128)}, u32[]{:S(2)}) copy-start(f32[8,768]{1,0:T(8,128)} %get-tuple-element.112) | copy-start | bytes 73732
  126.7 3.1 collective-permute-start.13
  130.8 12.5 %copy-start.48 = (bf16[768,1536]{1,0:T(8,128)(2,1)S(1)}, bf16[768,1536]{1,0:T(8,128)(2,1)}, u32[]{:S(2)}) copy-start(bf16[768,1536]{1,0:T(8,128)(2,1)} %get-tuple-element.115) | copy-start | bytes 7077892
  143.1 10.2 %collective-permute-start.14 = (bf16[768,768]{1,0:T(8,128)(2,1)}, bf16[768,768]{1,0:T(8,128)(2,1)S(1)}, u32[]{:S(2)}, u32[]{:S(2)}) collective-permute-start(bf16[768,768]{1,0:T(8,128)(2,1)} %get-tuple-element.107.mine), channel_id=1, source_target_pairs={{0,1},{1,0},{2,3},{3,2},{4,5},{5,4},{6,7},{7,6},{8,9},{9,8},{10,11... | collective-permute-start | bytes 3538952 | tf_op jit(solution)/shard_map/ppermute | solution.py:526
  147.6 30.4 %collective-permute-start.15 = (bf16[192,1536]{1,0:T(8,128)(2,1)S(1)}, bf16[192,1536]{1,0:T(8,128)(2,1)}, u32[]{:S(2)}, u32[]{:S(2)}) collective-permute-start(bf16[192,1536]{1,0:T(8,128)(2,1)S(1)} %get-tuple-element.180), channel_id=1, source_target_pairs={{0,8},{8,0},{16,24},{24,16},{1,9},{9,1},{17,25},{25,17},{2,10},{10... | collective-permute-start | bytes 1769480 | tf_op jit(solution)/shard_map/ppermute | solution.py:523
  148.2 30.6 %collective-permute-start.16 = (bf16[192,1536]{1,0:T(8,128)(2,1)S(1)}, bf16[192,1536]{1,0:T(8,128)(2,1)S(1)}, u32[]{:S(2)}, u32[]{:S(2)}) collective-permute-start(bf16[192,1536]{1,0:T(8,128)(2,1)S(1)} %get-tuple-element.179), channel_id=1, source_target_pairs={{0,16},{8,24},{16,0},{24,8},{1,17},{9,25},{17,1},{25,9},{2,18},{10... | collective-permute-start | bytes 1769480 | tf_op jit(solution)/shard_map/ppermute | solution.py:523
  149.7 29.7 %collective-permute-start.17 = (bf16[192,1536]{1,0:T(8,128)(2,1)}, bf16[192,1536]{1,0:T(8,128)(2,1)S(1)}, u32[]{:S(2)}, u32[]{:S(2)}) collective-permute-start(bf16[192,1536]{1,0:T(8,128)(2,1)} %get-tuple-element.178), channel_id=1, source_target_pairs={{0,24},{8,16},{16,8},{24,0},{1,25},{9,17},{17,9},{25,1},{2,26},{10... | collective-permute-start | bytes 1769480 | tf_op jit(solution)/shard_map/ppermute | solution.py:523
  162.8 14.0 %copy-start.37 = (f32[8,1536]{1,0:T(8,128)S(1)}, f32[8,1536]{1,0:T(8,128)}, u32[]{:S(2)}) copy-start(f32[8,1536]{1,0:T(8,128)} %get-tuple-element.122) | copy-start | bytes 147460
  164.0 38.5 %collective-permute-start.21 = (bf16[416,768]{1,0:T(8,128)(2,1)S(1)}, bf16[416,768]{1,0:T(8,128)(2,1)S(1)}, u32[]{:S(2)}, u32[]{:S(2)}) collective-permute-start(bf16[416,768]{1,0:T(8,128)(2,1)S(1)} %pad_maximum_fusion.17), channel_id=1, source_target_pairs={{0,2},{2,0},{4,6},{6,4},{1,3},{3,1},{5,7},{7,5},{8,10},{10,8},{12,... | collective-permute-start | bytes 1916936 | tf_op jit(solution)/shard_map/ppermute | solution.py:523
  175.7 78.4 %collective-permute-start.22 = (bf16[416,768]{1,0:T(8,128)(2,1)S(1)}, bf16[416,768]{1,0:T(8,128)(2,1)S(1)}, u32[]{:S(2)}, u32[]{:S(2)}) collective-permute-start(bf16[416,768]{1,0:T(8,128)(2,1)S(1)} %pad_maximum_fusion.17), channel_id=1, source_target_pairs={{0,4},{2,6},{4,0},{6,2},{1,5},{3,7},{5,1},{7,3},{8,12},{10,14},{12... | collective-permute-start | bytes 1916936 | tf_op jit(solution)/shard_map/ppermute | solution.py:523
  178.0 76.0 %collective-permute-start.23 = (bf16[416,768]{1,0:T(8,128)(2,1)S(1)}, bf16[416,768]{1,0:T(8,128)(2,1)S(1)}, u32[]{:S(2)}, u32[]{:S(2)}) collective-permute-start(bf16[416,768]{1,0:T(8,128)(2,1)S(1)} %pad_maximum_fusion.17), channel_id=1, source_target_pairs={{2,4},{4,2},{3,5},{5,3},{10,12},{12,10},{11,13},{13,11},{18,20},{2... | collective-permute-start | bytes 1916936 | tf_op jit(solution)/shard_map/ppermute | solution.py:555
  178.7 72.2 %copy-start.18 = (bf16[192,1536]{1,0:T(8,128)(2,1)}, bf16[192,1536]{1,0:T(8,128)(2,1)S(1)}, u32[]{:S(2)}) copy-start(bf16[192,1536]{1,0:T(8,128)(2,1)S(1)} %collective-permute-done.16) | copy-start | bytes 1769476
  178.8 75.9 %collective-permute-start.18 = (bf16[208,1536]{1,0:T(8,128)(2,1)S(1)}, bf16[208,1536]{1,0:T(8,128)(2,1)S(1)}, u32[]{:S(2)}, u32[]{:S(2)}) collective-permute-start(bf16[208,1536]{1,0:T(8,128)(2,1)S(1)} %get-tuple-element.238), channel_id=1, source_target_pairs={{0,8},{8,0},{16,24},{24,16},{1,9},{9,1},{17,25},{25,17},{2,10},{10... | collective-permute-start | bytes 1916936 | tf_op jit(solution)/shard_map/ppermute | solution.py:523
  179.4 24.7 %copy-start.20 = (bf16[192,1536]{1,0:T(8,128)(2,1)}, bf16[192,1536]{1,0:T(8,128)(2,1)S(1)}, u32[]{:S(2)}) copy-start(bf16[192,1536]{1,0:T(8,128)(2,1)S(1)} %collective-permute-done.17) | copy-start | bytes 1769476
  179.4 75.3 %collective-permute-start.19 = (bf16[208,1536]{1,0:T(8,128)(2,1)}, bf16[208,1536]{1,0:T(8,128)(2,1)}, u32[]{:S(2)}, u32[]{:S(2)}) collective-permute-start(bf16[208,1536]{1,0:T(8,128)(2,1)} %get-tuple-element.237), channel_id=1, source_target_pairs={{0,16},{8,24},{16,0},{24,8},{1,17},{9,25},{17,1},{25,9},{2,18},{10... | collective-permute-start | bytes 1916936 | tf_op jit(solution)/shard_map/ppermute | solution.py:523
  202.5 55.3 %copy-start.12 = (bf16[416,768]{1,0:T(8,128)(2,1)}, bf16[416,768]{1,0:T(8,128)(2,1)S(1)}, u32[]{:S(2)}) copy-start(bf16[416,768]{1,0:T(8,128)(2,1)S(1)} %collective-permute-done.21.refs_1_) | copy-start | bytes 1916932
  202.5 52.2 %collective-permute-start.20 = (bf16[208,1536]{1,0:T(8,128)(2,1)}, bf16[208,1536]{1,0:T(8,128)(2,1)}, u32[]{:S(2)}, u32[]{:S(2)}) collective-permute-start(bf16[208,1536]{1,0:T(8,128)(2,1)} %get-tuple-element.236), channel_id=1, source_target_pairs={{0,24},{8,16},{16,8},{24,0},{1,25},{9,17},{17,9},{25,1},{2,26},{10... | collective-permute-start | bytes 1916936 | tf_op jit(solution)/shard_map/ppermute | solution.py:523
  204.1 46.9 %copy-start.2 = (bf16[768,768]{1,0:T(8,128)(2,1)S(1)}, bf16[768,768]{1,0:T(8,128)(2,1)}, u32[]{:S(2)}) copy-start(bf16[768,768]{1,0:T(8,128)(2,1)} %get-tuple-element.128.refs_0_) | copy-start | bytes 3538948
  204.1 46.9 %copy-start.4 = (bf16[768,384]{1,0:T(8,128)(2,1)S(1)}, bf16[768,384]{1,0:T(8,128)(2,1)}, u32[]{:S(2)}) copy-start(bf16[768,384]{1,0:T(8,128)(2,1)} %get-tuple-element.93.att) | copy-start | bytes 1769476
  254.1 6.5 %collective-permute-start.24 = (bf16[416,768]{1,0:T(8,128)(2,1)S(1)}, bf16[416,768]{1,0:T(8,128)(2,1)S(1)}, u32[]{:S(2)}, u32[]{:S(2)}) collective-permute-start(bf16[416,768]{1,0:T(8,128)(2,1)S(1)} %collective-permute-done.21.refs_1_), channel_id=1, source_target_pairs={{0,1},{1,0},{2,3},{3,2},{4,5},{5,4},{6,7},{7,6},{8,9},{9,8},{10,11... | collective-permute-start | bytes 1916936 | tf_op jit(solution)/shard_map/ppermute | solution.py:526
  254.2 6.5 %collective-permute-start.25 = (bf16[416,768]{1,0:T(8,128)(2,1)S(1)}, bf16[416,768]{1,0:T(8,128)(2,1)S(1)}, u32[]{:S(2)}, u32[]{:S(2)}) collective-permute-start(bf16[416,768]{1,0:T(8,128)(2,1)S(1)} %collective-permute-done.22.refs_3_), channel_id=1, source_target_pairs={{0,1},{1,0},{2,3},{3,2},{4,5},{5,4},{6,7},{7,6},{8,9},{9,8},{10,11... | collective-permute-start | bytes 1916936 | tf_op jit(solution)/shard_map/ppermute | solution.py:526
  254.7 6.0 %collective-permute-start.26 = (bf16[416,768]{1,0:T(8,128)(2,1)S(1)}, bf16[416,768]{1,0:T(8,128)(2,1)S(1)}, u32[]{:S(2)}, u32[]{:S(2)}) collective-permute-start(bf16[416,768]{1,0:T(8,128)(2,1)S(1)} %collective-permute-done.23.refs_5_), channel_id=1, source_target_pairs={{0,1},{1,0},{2,3},{3,2},{4,5},{5,4},{6,7},{7,6},{8,9},{9,8},{10,11... | collective-permute-start | bytes 1916936 | tf_op jit(solution)/shard_map/ppermute | solution.py:526
  257.8 29.2 %collective-permute-start.28 = (bf16[112,1536]{1,0:T(8,128)(2,1)S(1)}, bf16[112,1536]{1,0:T(8,128)(2,1)S(1)}, u32[]{:S(2)}, u32[]{:S(2)}) collective-permute-start(bf16[112,1536]{1,0:T(8,128)(2,1)S(1)} %pad_maximum_fusion.21), channel_id=1, source_target_pairs={{0,2},{2,0},{4,6},{6,4},{1,3},{3,1},{5,7},{7,5},{8,10},{10,8},{12,... | collective-permute-start | bytes 1032200 | tf_op jit(solution)/shard_map/ppermute | solution.py:523
  257.9 29.3 %collective-permute-start.27 = (bf16[96,1536]{1,0:T(8,128)(2,1)S(1)}, bf16[96,1536]{1,0:T(8,128)(2,1)S(1)}, u32[]{:S(2)}, u32[]{:S(2)}) collective-permute-start(bf16[96,1536]{1,0:T(8,128)(2,1)S(1)} %get-tuple-element.198), channel_id=1, source_target_pairs={{0,2},{2,0},{4,6},{6,4},{1,3},{3,1},{5,7},{7,5},{8,10},{10,8},{12,... | collective-permute-start | bytes 884744 | tf_op jit(solution)/shard_map/ppermute | solution.py:523
  287.2 26.2 %copy-start.31 = (bf16[768,1152]{1,0:T(8,128)(2,1)S(1)}, bf16[768,1152]{1,0:T(8,128)(2,1)}, u32[]{:S(2)}) copy-start(bf16[768,1152]{1,0:T(8,128)(2,1)} %get-tuple-element.195) | copy-start | bytes 5308420
  287.2 26.2 %copy-start.34 = (bf16[768,128]{1,0:T(8,128)(2,1)S(1)}, bf16[768,128]{1,0:T(8,128)(2,1)}, u32[]{:S(2)}) copy-start(bf16[768,128]{1,0:T(8,128)(2,1)} %get-tuple-element.132) | copy-start | bytes 589828
  287.3 26.4 %collective-permute-start.29 = (bf16[96,1536]{1,0:T(8,128)(2,1)S(1)}, bf16[96,1536]{1,0:T(8,128)(2,1)S(1)}, u32[]{:S(2)}, u32[]{:S(2)}) collective-permute-start(bf16[96,1536]{1,0:T(8,128)(2,1)S(1)} %add_convert_fusion.7), channel_id=1, source_target_pairs={{0,4},{2,6},{4,0},{6,2},{1,5},{3,7},{5,1},{7,3},{8,12},{10,14},{12... | collective-permute-start | bytes 884744 | tf_op jit(solution)/shard_map/ppermute | solution.py:523
  311.4 14.1 %collective-permute-start.30 = (bf16[112,1536]{1,0:T(8,128)(2,1)S(1)}, bf16[112,1536]{1,0:T(8,128)(2,1)S(1)}, u32[]{:S(2)}, u32[]{:S(2)}) collective-permute-start(bf16[112,1536]{1,0:T(8,128)(2,1)S(1)} %pad_maximum_fusion.22), channel_id=1, source_target_pairs={{0,4},{2,6},{4,0},{6,2},{1,5},{3,7},{5,1},{7,3},{8,12},{10,14},{12... | collective-permute-start | bytes 1032200 | tf_op jit(solution)/shard_map/ppermute | solution.py:523
  313.8 53.3 %collective-permute-start.45 = (bf16[96,1536]{1,0:T(8,128)(2,1)S(1)}, bf16[96,1536]{1,0:T(8,128)(2,1)S(1)}, u32[]{:S(2)}, u32[]{:S(2)}) collective-permute-start(bf16[96,1536]{1,0:T(8,128)(2,1)S(1)} %add_convert_fusion.5), channel_id=1, source_target_pairs={{0,2},{2,0},{4,6},{6,4},{1,3},{3,1},{5,7},{7,5},{8,10},{10,8},{12,... | collective-permute-start | bytes 884744 | tf_op jit(solution)/shard_map/ppermute | solution.py:523
  325.6 17.7 %copy-start.32 = (bf16[768,128]{1,0:T(8,128)(2,1)S(1)}, bf16[768,128]{1,0:T(8,128)(2,1)}, u32[]{:S(2)}) copy-start(bf16[768,128]{1,0:T(8,128)(2,1)} %get-tuple-element.147) | copy-start | bytes 589828
  325.6 45.8 %collective-permute-start.44 = (bf16[96,1536]{1,0:T(8,128)(2,1)S(1)}, bf16[96,1536]{1,0:T(8,128)(2,1)S(1)}, u32[]{:S(2)}, u32[]{:S(2)}) collective-permute-start(bf16[96,1536]{1,0:T(8,128)(2,1)S(1)} %add_convert_fusion.4), channel_id=1, source_target_pairs={{0,2},{2,0},{4,6},{6,4},{1,3},{3,1},{5,7},{7,5},{8,10},{10,8},{12,... | collective-permute-start | bytes 884744 | tf_op jit(solution)/shard_map/ppermute | solution.py:523
  325.7 17.7 %copy-start.33 = (bf16[768,128]{1,0:T(8,128)(2,1)S(1)}, bf16[768,128]{1,0:T(8,128)(2,1)}, u32[]{:S(2)}) copy-start(bf16[768,128]{1,0:T(8,128)(2,1)} %get-tuple-element.148) | copy-start | bytes 589828
  347.0 5.9 %collective-permute-start.38 = (bf16[208,256]{1,0:T(8,128)(2,1)S(1)}, bf16[208,256]{1,0:T(8,128)(2,1)S(1)}, u32[]{:S(2)}, u32[]{:S(2)}) collective-permute-start(bf16[208,256]{1,0:T(8,128)(2,1)S(1)} %get-tuple-element.241), channel_id=1, source_target_pairs={{0,8},{8,0},{16,24},{24,16},{1,9},{9,1},{17,25},{25,17},{2,10},{10... | collective-permute-start | bytes 319496 | tf_op jit(solution)/shard_map/ppermute | solution.py:523
  347.1 7.2 %collective-permute-start.39 = (bf16[208,256]{1,0:T(8,128)(2,1)S(1)}, bf16[208,256]{1,0:T(8,128)(2,1)S(1)}, u32[]{:S(2)}, u32[]{:S(2)}) collective-permute-start(bf16[208,256]{1,0:T(8,128)(2,1)S(1)} %get-tuple-element.242), channel_id=1, source_target_pairs={{0,16},{8,24},{16,0},{24,8},{1,17},{9,25},{17,1},{25,9},{2,18},{10... | collective-permute-start | bytes 319496 | tf_op jit(solution)/shard_map/ppermute | solution.py:523
  347.2 7.1 %collective-permute-start.40 = (bf16[208,256]{1,0:T(8,128)(2,1)S(1)}, bf16[208,256]{1,0:T(8,128)(2,1)S(1)}, u32[]{:S(2)}, u32[]{:S(2)}) collective-permute-start(bf16[208,256]{1,0:T(8,128)(2,1)S(1)} %get-tuple-element.243), channel_id=1, source_target_pairs={{0,24},{8,16},{16,8},{24,0},{1,25},{9,17},{17,9},{25,1},{2,26},{10... | collective-permute-start | bytes 319496 | tf_op jit(solution)/shard_map/ppermute | solution.py:523
  352.9 18.6 %collective-permute-start.32 = (bf16[208,1280]{1,0:T(8,128)(2,1)S(1)}, bf16[208,1280]{1,0:T(8,128)(2,1)S(1)}, u32[]{:S(2)}, u32[]{:S(2)}) collective-permute-start(bf16[208,1280]{1,0:T(8,128)(2,1)S(1)} %get-tuple-element.227), channel_id=1, source_target_pairs={{0,8},{8,0},{16,24},{24,16},{1,9},{9,1},{17,25},{25,17},{2,10},{10... | collective-permute-start | bytes 1597448 | tf_op jit(solution)/shard_map/ppermute | solution.py:523
  354.3 23.5 %collective-permute-start.33 = (bf16[208,1280]{1,0:T(8,128)(2,1)S(1)}, bf16[208,1280]{1,0:T(8,128)(2,1)S(1)}, u32[]{:S(2)}, u32[]{:S(2)}) collective-permute-start(bf16[208,1280]{1,0:T(8,128)(2,1)S(1)} %get-tuple-element.226), channel_id=1, source_target_pairs={{0,16},{8,24},{16,0},{24,8},{1,17},{9,25},{17,1},{25,9},{2,18},{10... | collective-permute-start | bytes 1597448 | tf_op jit(solution)/shard_map/ppermute | solution.py:523
  354.4 4.4 %collective-permute-start.41 = (bf16[112,256]{1,0:T(8,128)(2,1)S(1)}, bf16[112,256]{1,0:T(8,128)(2,1)S(1)}, u32[]{:S(2)}, u32[]{:S(2)}) collective-permute-start(bf16[112,256]{1,0:T(8,128)(2,1)S(1)} %pad_maximum_fusion.34), channel_id=1, source_target_pairs={{0,2},{2,0},{4,6},{6,4},{1,3},{3,1},{5,7},{7,5},{8,10},{10,8},{12,... | collective-permute-start | bytes 172040 | tf_op jit(solution)/shard_map/ppermute | solution.py:523
  358.9 5.1 %collective-permute-start.42 = (bf16[112,256]{1,0:T(8,128)(2,1)S(1)}, bf16[112,256]{1,0:T(8,128)(2,1)S(1)}, u32[]{:S(2)}, u32[]{:S(2)}) collective-permute-start(bf16[112,256]{1,0:T(8,128)(2,1)S(1)} %pad_maximum_fusion.33), channel_id=1, source_target_pairs={{0,4},{2,6},{4,0},{6,2},{1,5},{3,7},{5,1},{7,3},{8,12},{10,14},{12... | collective-permute-start | bytes 172040 | tf_op jit(solution)/shard_map/ppermute | solution.py:523
  364.0 13.8 %collective-permute-start.34 = (bf16[208,1280]{1,0:T(8,128)(2,1)S(1)}, bf16[208,1280]{1,0:T(8,128)(2,1)S(1)}, u32[]{:S(2)}, u32[]{:S(2)}) collective-permute-start(bf16[208,1280]{1,0:T(8,128)(2,1)S(1)} %get-tuple-element.225), channel_id=1, source_target_pairs={{0,24},{8,16},{16,8},{24,0},{1,25},{9,17},{17,9},{25,1},{2,26},{10... | collective-permute-start | bytes 1597448 | tf_op jit(solution)/shard_map/ppermute | solution.py:523
  367.0 4.3 %collective-permute-start.43 = (bf16[96,256]{1,0:T(8,128)(2,1)S(1)}, bf16[96,256]{1,0:T(8,128)(2,1)S(1)}, u32[]{:S(2)}, u32[]{:S(2)}) collective-permute-start(bf16[96,256]{1,0:T(8,128)(2,1)S(1)} %add_convert_fusion.10), channel_id=1, source_target_pairs={{0,2},{2,0},{4,6},{6,4},{1,3},{3,1},{5,7},{7,5},{8,10},{10,8},{12,... | collective-permute-start | bytes 147464 | tf_op jit(solution)/shard_map/ppermute | solution.py:523
  371.4 28.3 %collective-permute-start.31 = (bf16[768,768]{1,0:T(8,128)(2,1)S(1)}, bf16[768,768]{1,0:T(8,128)(2,1)S(1)}, u32[]{:S(2)}, u32[]{:S(2)}) collective-permute-start(bf16[768,768]{1,0:T(8,128)(2,1)S(1)} %convolution_convert_fusion.3), channel_id=1, source_target_pairs={{0,1},{1,0},{2,3},{3,2},{4,5},{5,4},{6,7},{7,6},{8,9},{9,8},{10,11... | collective-permute-start | bytes 3538952 | tf_op jit(solution)/shard_map/ppermute | solution.py:526
  378.2 9.8 %collective-permute-start.35 = (bf16[112,1280]{1,0:T(8,128)(2,1)S(1)}, bf16[112,1280]{1,0:T(8,128)(2,1)S(1)}, u32[]{:S(2)}, u32[]{:S(2)}) collective-permute-start(bf16[112,1280]{1,0:T(8,128)(2,1)S(1)} %pad_maximum_fusion.20), channel_id=1, source_target_pairs={{0,2},{2,0},{4,6},{6,4},{1,3},{3,1},{5,7},{7,5},{8,10},{10,8},{12,... | collective-permute-start | bytes 860168 | tf_op jit(solution)/shard_map/ppermute | solution.py:523
  379.3 20.3 %copy-start.5 = (f32[768,768]{1,0:T(8,128)S(1)}, f32[768,768]{1,0:T(8,128)}, u32[]{:S(2)}) copy-start(f32[768,768]{1,0:T(8,128)} %get-tuple-element.110) | copy-start | bytes 7077892
  388.1 10.7 %collective-permute-start.36 = (bf16[112,1280]{1,0:T(8,128)(2,1)S(1)}, bf16[112,1280]{1,0:T(8,128)(2,1)S(1)}, u32[]{:S(2)}, u32[]{:S(2)}) collective-permute-start(bf16[112,1280]{1,0:T(8,128)(2,1)S(1)} %pad_maximum_fusion.19), channel_id=1, source_target_pairs={{0,4},{2,6},{4,0},{6,2},{1,5},{3,7},{5,1},{7,3},{8,12},{10,14},{12... | collective-permute-start | bytes 860168 | tf_op jit(solution)/shard_map/ppermute | solution.py:523
  398.9 6.3 %collective-permute-start.37 = (bf16[96,1280]{1,0:T(8,128)(2,1)S(1)}, bf16[96,1280]{1,0:T(8,128)(2,1)S(1)}, u32[]{:S(2)}, u32[]{:S(2)}) collective-permute-start(bf16[96,1280]{1,0:T(8,128)(2,1)S(1)} %add_convert_fusion.8), channel_id=1, source_target_pairs={{0,2},{2,0},{4,6},{6,4},{1,3},{3,1},{5,7},{7,5},{8,10},{10,8},{12,... | collective-permute-start | bytes 737288 | tf_op jit(solution)/shard_map/ppermute | solution.py:523
  (33 other events, 92.5 us)
where the time goes:
time: 406 us; the launch traced here: 407 us
  Pallas kernels  183 us (45%)
  waiting for transfers between devices  106 us (26%)
  starting transfers between devices  66.1 us (16%)
  local copies, waits for them, and re-layouts  20.4 us (5%)
  other arithmetic  16.4 us (4%)
  matrix products  11.8 us (3%)
    ppermute x34, waiting for transfers between devices, partner(): return lax.ppermute(value, axis, [(i, i ^ d) for i in range(4)])  101 us
    ppermute x34, starting transfers between devices, partner(): return lax.ppermute(value, axis, [(i, i ^ d) for i in range(4)])  62.1 us
    pallas_call x3, Pallas kernels, key_grads(): pl.pallas_call(kernel, grid_spec=pltpu.PrefetchScalarGridSpec(num_scalar_...  49.1 us
    pallas_call x1, Pallas kernels, query_grads(): pl.pallas_call(query_kernel, grid_spec=pltpu.PrefetchScalarGridSpec(num_s...  46.9 us
    pallas_call x3, Pallas kernels, call_rows(): pl.pallas_call(kernel, grid=(rows // BQ,), in_specs=specs, out_specs=out_...  30.9 us
    pallas_call x1, Pallas kernels, attend(): pl.pallas_call(attend_kernel, grid_spec=pltpu.PrefetchScalarGridSpec(num_...  29.5 us
    pallas_call x2, Pallas kernels, project(): pl.pallas_call(kernel, grid_spec=pltpu.PrefetchScalarGridSpec(num_scalar_...  20.7 us
    dot_general x7, matrix products, dot(): return lax.dot_general(a, b, dims, preferred_element_type=F32)  11.8 us
  transfers between devices with their start and end apart: 46, of which 18 were waited for; matrix products, arithmetic and copies ran while one was open for 9% of the time, Pallas kernels for 38%

commit v1 on v0

--- a/solution.py
+++ b/solution.py
@@ -89,7 +89,7 @@
         nxt = p + 1
         if nxt < pairs:
             ahead = slice(nxt * 128, nxt * 128 + 128)
-            heads = [pick(q_ref[:, ahead], side) for side in range(2)]
+            heads = [jnp.transpose(pick(q_ref[:, ahead], side)) for side in range(2)]
         here = slice(p * 128, p * 128 + 128)
 
         def body(j, carry):
@@ -98,7 +98,7 @@
             if nxt < pairs:
                 keys = k_ref[rows, ahead]
                 for side in range(2):
-                    s = dot(keys, heads[side], ROW) + bias[j]
+                    s = dot(keys, heads[side]) + bias[j]
                     score[nxt % 2, side, j] = s
                     tops[side] = jnp.maximum(tops[side], jnp.max(s.reshape(BK // 8, 8, BQ), axis=0))
             if p >= 0:
@@ -174,8 +174,8 @@
             h = 2 * p + side
             sides.append(
                 (
-                    pick(q_ref[:, span], side),
-                    pick(do_ref[:, span], side),
+                    jnp.transpose(pick(q_ref[:, span], side)),
+                    jnp.transpose(pick(do_ref[:, span], side)),
                     stat_ref[8 + h : 9 + h, :],
                     stat_ref[h : h + 1, :],
                 )
@@ -189,8 +189,8 @@
             out = []
             for side in range(2):
                 qh, gh, delta, lse = sides[side]
-                prob = jnp.exp2(dot(keys, qh, ROW) + bias[j] - lse)
-                score = (prob * (dot(values, gh, ROW) - delta)).astype(BF16)
+                prob = jnp.exp2(dot(keys, qh) + bias[j] - lse)
+                score = (prob * (dot(values, gh) - delta)).astype(BF16)
                 out.append(accs[side] + dot(turned[64 * side : 64 * side + 64], score))
             return tuple(out)
 
@@ -233,32 +233,40 @@
     first = s_ref[2] + pl.program_id(0) * BK
     lo, hi = key_range(first, first + BK - 1, b1, b2, total)
     j0, j1 = lo // BQ, (hi + BQ - 1) // BQ
-    rows = first + lax.broadcasted_iota(jnp.int32, (BK, 1), 0)
-    row_seg = segment_of(rows, b1, b2)
-    masked = column(mask_ref[0])
+    cols = first + lax.broadcasted_iota(jnp.int32, (1, BK), 1)
+    col_seg = segment_of(cols, b1, b2)
+    masked = jnp.broadcast_to(mask_ref[0], (BQ, BK))
+    sides = [
+        (jnp.transpose(pick(k_ref[...], side)), jnp.transpose(pick(v_ref[...], side)))
+        for side in range(2)
+    ]
 
     def body(j, carry):
-        dk, dv = carry
         span = pl.ds(pl.multiple_of(j * BQ, BQ), BQ)
-        cols = j * BQ + lax.broadcasted_iota(jnp.int32, (1, BQ), 1)
-        col_seg = segment_of(cols, b1, b2)
+        rows = j * BQ + lax.broadcasted_iota(jnp.int32, (BQ, 1), 0)
+        row_seg = segment_of(rows, b1, b2)
         bias = jnp.where(row_seg == col_seg, jnp.where(rows == cols, 0.0, masked), NEG)
         queries, grads = q_ref[span, :], do_ref[span, :]
+        qt, gt = jnp.transpose(queries), jnp.transpose(grads)
         place = ((j // per) ^ s_ref[3]) * per + lax.rem(j, per)
-        spot = pl.ds(pl.multiple_of(place * BQ, BQ), BQ)
+        stats = jnp.transpose(stat_ref[:, pl.ds(pl.multiple_of(place * BQ, BQ), BQ)])
+        out = []
         for side in range(2):
             h = 2 * pair + side
-            qh, gh = pick(queries, side), pick(grads, side)
-            prob = jnp.exp2(dot(k_ref[...], qh, ROW) + bias - stat_ref[h : h + 1, spot])
-            score = prob * (dot(v_ref[...], gh, ROW) - stat_ref[8 + h : 9 + h, spot])
-            dk = dk + dot(score.astype(BF16), qh)
-            dv = dv + dot(prob.astype(BF16), gh)
-        return dk, dv
-
-    zero = jnp.zeros((BK, 128), F32)
-    dk, dv = lax.fori_loop(j0, j1, body, (zero, zero))
-    dk_ref[...] = (dk * (1.0 / LOG2E)).astype(BF16)
-    dv_ref[...] = dv.astype(BF16)
+            kh, vh = sides[side]
+            part = slice(64 * side, 64 * side + 64)
+            dk, dv = carry[side]
+            prob = jnp.exp2(dot(queries, kh) + bias - stats[:, h : h + 1])
+            score = prob * (dot(grads, vh) - stats[:, 8 + h : 9 + h])
+            out.append(
+                (dk + dot(qt[part], score.astype(BF16)), dv + dot(gt[part], prob.astype(BF16)))
+            )
+        return tuple(out)
+
+    zero = jnp.zeros((64, BK), F32)
+    (k0, v0), (k1, v1) = lax.fori_loop(j0, j1, body, ((zero, zero), (zero, zero)))
+    dk_ref[...] = (jnp.transpose(jnp.concatenate([k0, k1], axis=0)) * (1.0 / LOG2E)).astype(BF16)
+    dv_ref[...] = jnp.transpose(jnp.concatenate([v0, v1], axis=0)).astype(BF16)
 
 
 def key_grads(scalars, qkv, dout, stats, kb, rows, pairs, pair):
@@ -392,6 +400,88 @@
         ),
         name="project",
     )(scalars, *pieces, *weights, *extra)
+
+
+def project_slots(scalars, slots, weights, wspots, bias, scale, total, whole=None):
+    rows, depth = slots[0][1][0].shape[0] * len(slots[0][1]), slots[0][1][0].shape[1]
+    pieces = [piece for _, group in slots for piece in group]
+    count, wcount = len(pieces), len(weights)
+    cols = bias.shape[1]
+    fresh = whole is None
+    offsets = [d for d, _ in slots]
+
+    def kernel(s_ref, *refs):
+        ins, ws = refs[:count], refs[count : count + wcount]
+        bias_ref, scale_ref = refs[count + wcount : count + wcount + 2]
+        rest = refs[count + wcount + 2 :]
+        if fresh:
+            out_ref, w_ref, x_ref = rest
+        else:
+            _, out_ref, x_ref = rest
+            w_ref = ws[0]
+        step = pl.program_id(0)
+        if fresh:
+
+            @pl.when(step == 0)
+            def _():
+                for i in range(wcount):
+                    height, start = wspots[i](s_ref)
+                    put(w_ref, ws[i], height, start)
+
+        seen = 0
+        for k, (_, group) in enumerate(slots):
+            own = ins[seen : seen + len(group)]
+            seen += len(group)
+
+            @pl.when(step == k)
+            def _(own=own):
+                if len(own) == 1:
+                    x_ref[...] = own[0][...]
+                else:
+                    half = rows // 2
+                    put(x_ref, own[0], half, s_ref[5] * half)
+                    put(x_ref, own[1], half, (1 - s_ref[5]) * half)
+
+        value = (dot(x_ref[...], w_ref[...]) + bias_ref[...]) * scale_ref[...]
+        out_ref[...] = value.astype(BF16)
+
+    def spot(i, s):
+        d = offsets[0]
+        for k in range(1, len(offsets)):
+            d = jnp.where(i == k, offsets[k], d)
+        return (s[4] ^ d, 0)
+
+    operands = pieces + weights + [bias, scale]
+    in_specs = [whole_spec(value) for value in operands]
+    out_specs = [pl.BlockSpec((rows, cols), spot)]
+    out_shape = [jax.ShapeDtypeStruct((total, cols), BF16)]
+    aliases = {}
+    if fresh:
+        out_specs.append(pl.BlockSpec((depth, cols), lambda i, s: (0, 0)))
+        out_shape.append(jax.ShapeDtypeStruct((depth, cols), BF16))
+    else:
+        aliases = {1 + len(operands): 0}
+        operands = operands + [whole]
+        in_specs.append(pl.BlockSpec(memory_space=pl.ANY))
+    return pl.pallas_call(
+        kernel,
+        grid_spec=pltpu.PrefetchScalarGridSpec(
+            num_scalar_prefetch=1,
+            grid=(len(slots),),
+            in_specs=in_specs,
+            out_specs=out_specs,
+            scratch_shapes=[pltpu.VMEM((rows, depth), BF16)],
+        ),
+        out_shape=out_shape,
+        input_output_aliases=aliases,
+        compiler_params=pltpu.CompilerParams(
+            dimension_semantics=("arbitrary",), vmem_limit_bytes=LIMIT
+        ),
+        cost_estimate=pl.CostEstimate(
+            flops=2 * len(slots) * rows * depth * cols, transcendentals=0, bytes_accessed=4_000_000
+        ),
+        name="project_slots",
+    )(scalars, *operands)
 
 
 def call_rows(kernel, rows, name, blocked, fixed, outs, kept=(), flops=0):
@@ -686,17 +776,28 @@
 
         got = send_rows(tokens)
         wq = send_weight(w_qkv, 1)
-        got, wq = lax.optimization_barrier((got, wq))
         shard = jnp.concatenate([w_attn_out.T, w_up, w_down.T], axis=1)
-        rest = send_weight(after(shard, wq[-1]))
+        rest = send_weight(after(shard, wq[min(1, len(wq) - 1)]))
         cuts = [(0, width), (width, hidden), (width + hidden, hidden)]
         zero = jnp.zeros((width,), F32)
         bias_row = jnp.concatenate([bias_qv[0], zero, bias_qv[1]]).reshape(1, -1)
         scale_row = jnp.concatenate([zero + 0.125 * LOG2E, zero + 1.0, zero + 1.0]).reshape(1, -1)
-        pieces, spots = row_pieces(tokens, got)
-        qkv, w_proj = project(
-            scalars, pieces, spots, total, wq, weight_spots(wq, 1), bias_row, scale_row
-        )
+        if direct_c:
+            near, far, inner = got
+            (near, inner), wq = lax.optimization_barrier(((near, inner), wq))
+            slots = [(0, [tokens]), (1, [near, twin(near)]), (3, [inner, twin(inner)])]
+            qkv, w_proj = project_slots(
+                scalars, slots, wq, weight_spots(wq, 1), bias_row, scale_row, total
+            )
+            far = after(far, w_proj)
+            (qkv,) = project_slots(
+                scalars, [(2, [far, twin(far)])], [w_proj], None, bias_row, scale_row, total, qkv
+            )
+        else:
+            pieces, spots = row_pieces(tokens, got)
+            qkv, w_proj = project(
+                scalars, pieces, spots, total, wq, weight_spots(wq, 1), bias_row, scale_row
+            )
         attended, lset = attend(scalars, qkv, kb, rows, pairs)
         rest = after(rest, attended)
         w_back, w_upper, w_lower = place(scalars, rest, weight_spots(rest), dim, cuts)
@@ -723,7 +824,8 @@
             flops=work,
         )
         other = twin(part)
-        group_a, _ = send_f([dot(lower_grad.T, active).astype(BF16)])
+        grad_low = dot(lower_grad.T, active).astype(BF16)
+        grad_up = dot(first_low.T, grad_upper).astype(BF16)
         grad_first_sum, branch_grad, dout, deltat, small = call_rows(
             branch_kernel,
             rows,
@@ -736,77 +838,70 @@
         )
         stats = jnp.concatenate([lset, deltat], axis=0)
         got = send_rows(branch_grad, stats)
-        group_b, small = send_f([dot(first_low.T, grad_upper).astype(BF16)], small)
+        small = jnp.pad(small, ((0, 0), (0, hidden + width)))
+        grad_back = dot(branch_grad.T, attended).astype(BF16)
+        group_a, small = send_f([grad_low, grad_up, grad_back], small)
         dq = query_grads(scalars, qkv, dout, stats, kb, rows, pairs)
 
         got = after(got, dq)
         stats_all = row_stats(stats, got, rows // 2)
         pieces, spots = row_pieces(branch_grad, got)
         (dout_all,) = project(scalars, pieces, spots, total, [w_back], None)
-        group_a, _ = finish_f(after(group_a, dq))
-        group_b, small = finish_f(after(group_b, dq), small)
-        state_a, state_b = send_1(group_a), send_1(group_b, small)
+        group_a, small = finish_f(after(group_a, dq), small)
+        state_a = send_1(group_a, small)
         dks, dvs = [], []
-        gate = (group_a, group_b)
+        gate = group_a
         for pair in range(pairs):
             dk, dv = key_grads(
                 after(scalars, gate), qkv, dout_all, stats_all, kb, rows, pairs, pair
             )
             dks.append(dk)
             dvs.append(dv)
+            gate = dk
             if pair == 0:
-                group_a, group_b = finish_z(after(state_a, dk)), finish_z(after(state_b, dk))
-                state_a, state_b = send_2(*group_a), send_2(*group_b)
-                gate = (group_a, group_b)
+                state_a = finish_z(after(state_a, dk))
+                gate = state_a
+                state_a = send_2(*state_a)
             elif pair == 1:
-                group_a, group_b = finish_z(after(state_a, dk)), finish_z(after(state_b, dk))
-                state_a, state_b = send_3(*group_a), send_3(*group_b)
                 early = jnp.concatenate([dq] + dks + dvs, axis=1)
-                sums = jnp.sum(early.astype(F32), axis=0, keepdims=True)
-                row = jnp.pad(sums, ((0, 0), (0, width)))
-                group_c, row = send_f(
-                    [
-                        dot(tokens.T, early).astype(BF16),
-                        dot(branch_grad.T, attended).astype(BF16),
-                    ],
-                    row,
-                )
-                gate = (group_a, group_b)
+                row = jnp.sum(early.astype(F32), axis=0, keepdims=True)
+                group_c, row = send_f([dot(tokens.T, early).astype(BF16)], row)
         late = jnp.concatenate([dks[-1], dvs[-1]], axis=1)
         tail = jnp.sum(late.astype(F32), axis=0, keepdims=True)
         group_d, tail = send_f([dot(tokens.T, late).astype(BF16)], tail)
         group_c, row = finish_f(after(group_c, late), row)
-        state_c = send_1(group_c, row)
+        state_a = send_3(*finish_z(after(state_a, late)))
         stacked = jnp.concatenate([dq] + dks + dvs, axis=1)
         input_part = pair_sum(dot(stacked, w_proj, ROW))
         grad_tokens = (grad_first_sum + input_part).astype(BF16)
         group_d, tail = finish_f(group_d, tail)
-        state_d = send_1(group_d, tail)
-        state_c, state_d = send_2(*finish_z(state_c)), send_2(*finish_z(state_d))
-        group_a, _ = finish_3(after(state_a, late))
-        group_b, small = finish_3(after(state_b, late))
-        state_c, state_d = send_3(*finish_z(state_c)), send_3(*finish_z(state_d))
+        both = jnp.concatenate([group_c, group_d], axis=1)
+        row = jnp.concatenate([row, tail], axis=1)
+        state_c = send_2(*finish_z(send_1(both, row)))
+        group_a, small = finish_3(state_a)
+        state_c = send_3(*finish_z(state_c))
         group_c, row = finish_3(state_c)
-        group_d, tail = finish_3(state_d)
-
-        sum_gains = jnp.stack([small[0, dim:], small[0, :dim]])
-        sum_shifts = jnp.stack([small[2, dim:], small[1, dim:], small[2, :dim], small[1, :dim]])
-        sum_bias_up = small[3]
-        near_k = width + width - 128
-        near_v = near_k + width - 128
+
+        sum_gains = jnp.stack([small[0, dim : 2 * dim], small[0, :dim]])
+        sum_shifts = jnp.stack(
+            [small[2, dim : 2 * dim], small[1, dim : 2 * dim], small[2, :dim], small[1, :dim]]
+        )
+        sum_bias_up = small[3, :hidden]
+        low_k = 2 * width - 128
+        low_v = low_k + width - 128
         sum_bias_qv = jnp.stack(
-            [row[0, :width], jnp.concatenate([row[0, near_k:near_v], tail[0, 128:]])]
+            [row[0, :width], jnp.concatenate([row[0, low_k:low_v], row[0, low_v + 128 :]])]
         )
         share_qkv = jnp.stack(
             [
                 group_c[:, :width],
-                jnp.concatenate([group_c[:, width:near_k], group_d[:, :128]], axis=1),
-                jnp.concatenate([group_c[:, near_k:near_v], group_d[:, 128:]], axis=1),
+                jnp.concatenate([group_c[:, width:low_k], group_c[:, low_v : low_v + 128]], axis=1),
+                jnp.concatenate([group_c[:, low_k:low_v], group_c[:, low_v + 128 :]], axis=1),
             ]
         )
-        share_lower = group_a.T
-        share_upper = group_b
-        share_back = group_c[:, near_v:].T
+        share_lower = group_a[:, :hidden].T
+        share_upper = group_a[:, hidden : 2 * hidden]
+        share_back = group_a[:, 2 * hidden :].T
         return (
             out,
             grad_tokens,

time: 406 us -> 435 us (1.071)
  waiting for transfers between devices: 106 us -> 152 us
  Pallas kernels: 183 us -> 160 us
  starting transfers between devices: 66.1 us -> 70.5 us
    ppermute x34 -> x25, waiting for transfers between devices: 101 us -> 146 us  [partner(): return lax.ppermute(value, axis, [(i, i ^ d) for i in range(4)])]
    pallas_call x0 -> x2, Pallas kernels: none -> 15.6 us  [project_slots(): pl.pallas_call(kernel, grid_spec=pltpu.PrefetchScalarGridSpec(num_scalar_...]
    pallas_call x2 -> x1, Pallas kernels: 20.7 us -> 8.19 us  [project(): pl.pallas_call(kernel, grid_spec=pltpu.PrefetchScalarGridSpec(num_scalar_...]
    pallas_call x1, Pallas kernels: 46.9 us -> 35 us  [query_grads(): pl.pallas_call(query_kernel, grid_spec=pltpu.PrefetchScalarGridSpec(num_s...]
    pallas_call x3, Pallas kernels: 49.1 us -> 41.7 us  [key_grads(): pl.pallas_call(kernel, grid_spec=pltpu.PrefetchScalarGridSpec(num_scalar_...]
    pallas_call x1, Pallas kernels: 29.5 us -> 22.6 us  [attend(): pl.pallas_call(attend_kernel, grid_spec=pltpu.PrefetchScalarGridSpec(num_...]
    ppermute x34 -> x25, starting transfers between devices: 62.1 us -> 67.6 us  [partner(): return lax.ppermute(value, axis, [(i, i ^ d) for i in range(4)])]
    unnamed x108 -> x102, local copies, waits for them, and re-layouts: 9.65 us -> 12.5 us
  transfers between devices with their start and end apart: 46 -> 37, of which waited for: 18 -> 19; matrix products, arithmetic and copies ran while one was open for 9% -> 6% of each run, Pallas kernels for 38% -> 22%
where the time goes in v1:
time: 435 us
  Pallas kernels  160 us (37%)
  waiting for transfers between devices  152 us (35%)
  starting transfers between devices  70.5 us (16%)
  local copies, waits for them, and re-layouts  22.3 us (5%)
  other arithmetic  15.8 us (4%)
  matrix products  11.9 us (3%)
    ppermute x25, waiting for transfers between devices, partner(): return lax.ppermute(value, axis, [(i, i ^ d) for i in range(4)])  146 us
    ppermute x25, starting transfers between devices, partner(): return lax.ppermute(value, axis, [(i, i ^ d) for i in range(4)])  67.6 us
    pallas_call x3, Pallas kernels, key_grads(): pl.pallas_call(kernel, grid_spec=pltpu.PrefetchScalarGridSpec(num_scalar_...  41.7 us
    pallas_call x1, Pallas kernels, query_grads(): pl.pallas_call(query_kernel, grid_spec=pltpu.PrefetchScalarGridSpec(num_s...  35 us
    pallas_call x3, Pallas kernels, call_rows(): pl.pallas_call(kernel, grid=(rows // BQ,), in_specs=specs, out_specs=out_...  30.9 us
    pallas_call x1, Pallas kernels, attend(): pl.pallas_call(attend_kernel, grid_spec=pltpu.PrefetchScalarGridSpec(num_...  22.6 us
    pallas_call x2, Pallas kernels, project_slots(): pl.pallas_call(kernel, grid_spec=pltpu.PrefetchScalarGridSpec(num_scalar_...  15.6 us
    unnamed x102, local copies, waits for them, and re-layouts  12.5 us
  transfers between devices with their start and end apart: 37, of which 19 were waited for; matrix products, arithmetic and copies ran while one was open for 6% of the time, Pallas kernels for 22%

profile of v1, /device:TPU:0, one launch (start us, length us, event | category | flops | bytes accessed | tf_op | source)
XLA Modules:
  0.0 435.1 jit_solution(13927509173490096919)
XLA Ops:
  0.6 1.1 constant_dynamic-slice_fusion.15
  1.8 3.1 collective-permute-start.1
  5.6 1.6 collective-permute-start.3
  7.1 1.5 collective-permute-start.4
  9.1 9.8 %collective-permute-done.3.refs_6_ = bf16[3,192,384]{2,1,0:T(8,128)(2,1)S(1)} collective-permute-done((bf16[3,192,384]{2,1,0:T(8,128)(2,1)}, bf16[3,192,384]{2,1,0:T(8,128)(2,1)S(1)}, u32[]{:S(2)}, u32[]{:S(2)}) %collective-permute-start.3) | collective-permute-done | bytes 442400 | tf_op jit(solution)/shard_map/ppermute | solution.py:613
  18.9 9.3 %collective-permute-done.4.refs_7_ = bf16[3,192,384]{2,1,0:T(8,128)(2,1)S(1)} collective-permute-done((bf16[3,192,384]{2,1,0:T(8,128)(2,1)}, bf16[3,192,384]{2,1,0:T(8,128)(2,1)S(1)}, u32[]{:S(2)}, u32[]{:S(2)}) %collective-permute-start.4) | collective-permute-done | bytes 442400 | tf_op jit(solution)/shard_map/ppermute | solution.py:613
  29.2 3.8 collective-permute-start
  34.4 1.3 fusion.32
  37.0 1.3 stack.48.s_ref.refs_0_
  39.9 10.1 %project_slots.2 = (bf16[3072,1152]{1,0:T(8,128)(2,1)}, bf16[768,1152]{1,0:T(8,128)(2,1)}) custom-call(s32[7]{0:T(128)} %stack.48.s_ref.refs_0_, bf16[768,768]{1,0:T(8,128)(2,1)} %tok.1, bf16[384,768]{1,0:T(8,128)(2,1)} %copy-done.39, bf16[384,768]{1,0:T(8,128)(2,1)} %copy-done.41, bf16[384,768]{1,0:T(8,128)(2,1)} %copy-done.40, ...), custom_call_target="tpu_custom_call" | custom-call | flops 4076863488 | bytes 4000000 | tf_op jit(solution)/shard_map/project_slots/pallas_call | solution.py:466
  50.0 8.8 %collective-permute-done.refs_0_ = bf16[384,768]{1,0:T(8,128)(2,1)S(1)} collective-permute-done((bf16[384,768]{1,0:T(8,128)(2,1)S(1)}, bf16[384,768]{1,0:T(8,128)(2,1)S(1)}, u32[]{:S(2)}, u32[]{:S(2)}) %collective-permute-start) | collective-permute-done | bytes 589856 | tf_op jit(solution)/shard_map/ppermute | solution.py:613
  59.6 1.6 collective-permute-start.10
  61.2 1.2 collective-permute-start.11
  64.0 5.5 %project_slots.3.q_ref.k_ref.v_ref.refs_1_.refs_2_.refs_3_ = bf16[3072,1152]{1,0:T(8,128)(2,1)} custom-call(s32[7]{0:T(128)} %stack.48.s_ref.refs_0_, bf16[384,768]{1,0:T(8,128)(2,1)} %copy-done.19, bf16[384,768]{1,0:T(8,128)(2,1)} %copy-done.20, bf16[768,1152]{1,0:T(8,128)(2,1)} %get-tuple-element.78.refs_2_, ...), custom_call_target="tpu_custom_call", output_to_operand_aliasing={{}: (6, {})} | custom-call | flops 1358954496 | bytes 4000000 | tf_op jit(solution)/shard_map/project_slots/pallas_call | solution.py:466
  69.5 22.6 %attend.1 = (bf16[768,384]{1,0:T(8,128)(2,1)}, f32[8,768]{1,0:T(8,128)}) custom-call(s32[7]{0:T(128)} %stack.48.s_ref.refs_0_, bf16[3072,1152]{1,0:T(8,128)(2,1)} %project_slots.3.q_ref.k_ref.v_ref.refs_1_.refs_2_.refs_3_, bf16[3072,1152]{1,0:T(8,128)(2,1)} %project_slots.3.q_ref.k_ref.v_ref.refs_1_.refs_2_.refs_3_, ...), custom_call_target="tpu_custom_call" | custom-call | flops 35999997952 | bytes 8000000 | tf_op jit(solution)/shard_map/attend/pallas_call | solution.py:130
  92.1 27.6 %collective-permute-done.10.refs_2_ = bf16[192,3456]{1,0:T(8,128)(2,1)S(1)} collective-permute-done((bf16[192,3456]{1,0:T(8,128)(2,1)S(1)}, bf16[192,3456]{1,0:T(8,128)(2,1)S(1)}, u32[]{:S(2)}, u32[]{:S(2)}) %collective-permute-start.10) | collective-permute-done | bytes 1327136 | tf_op jit(solution)/shard_map/ppermute | solution.py:613
  119.6 1.2 collective-permute-done.9.refs_1_
  121.9 5.9 %place.1 = (bf16[768,384]{1,0:T(8,128)(2,1)}, bf16[768,1536]{1,0:T(8,128)(2,1)}, bf16[768,1536]{1,0:T(8,128)(2,1)}) custom-call(s32[7]{0:T(128)} %stack.48.s_ref.refs_0_, bf16[192,3456]{1,0:T(8,128)(2,1)} %copy-done, bf16[192,3456]{1,0:T(8,128)(2,1)} %copy-done.9, bf16[192,3456]{1,0:T(8,128)(2,1)} %copy-done.7, bf16[192,3456]{1,0:T(8,128)(2,1)} %copy-done.8), custom_call_target="tpu_custom_call" | custom-call | tf_op jit(solution)/shard_map/place/pallas_call | solution.py:331
  127.9 1.9 convolution_convert_fusion.4.mine
  130.5 2.1 collective-permute-done.12.other
  132.7 1.0 copy-done.38
  133.7 10.9 %upper.1 = (f32[768,768]{1,0:T(8,128)}, f32[768,128]{1,0:T(8,128)}, bf16[768,768]{1,0:T(8,128)(2,1)}, bf16[768,1536]{1,0:T(8,128)(2,1)}, f32[768,1536]{1,0:T(8,128)}, /*index=5*/bf16[768,768]{1,0:T(8,128)(2,1)}) custom-call(bf16[768,768]{1,0:T(8,128)(2,1)} %tok.1, bf16[768,768]{1,0:T(8,128)(2,1)} %copy-done.12, bf16[768,768]{1,0:T(8,128)(2,1)} %copy-done.38, ...), custom_call_target="tpu_custom_call" | custom-call | flops 7247757312 | bytes 4000000 | tf_op jit(solution)/shard_map/upper/pallas_call | solution.py:501
  145.5 2.2 collective-permute-done.13.other
  147.7 1.0 copy-done.10
  148.7 12.5 %lower.1 = (bf16[768,768]{1,0:T(8,128)(2,1)}, f32[768,768]{1,0:T(8,128)}, bf16[768,768]{1,0:T(8,128)(2,1)}, bf16[768,1536]{1,0:T(8,128)(2,1)}, bf16[768,768]{1,0:T(8,128)(2,1)}, /*index=5*/f32[8,1536]{1,0:T(8,128)}) custom-call(f32[768,768]{1,0:T(8,128)} %get-tuple-element.90.normed_ref, bf16[768,768]{1,0:T(8,128)(2,1)} %get-tuple-element.91.mine, ...), custom_call_target="tpu_custom_call" | custom-call | flops 3623878656 | bytes 4000000 | tf_op jit(solution)/shard_map/lower/pallas_call | solution.py:501
  161.4 3.4 convolution_convert_fusion.1
  164.9 2.0 convolution_convert_fusion
  168.3 7.5 %branch.1 = (f32[768,768]{1,0:T(8,128)}, bf16[768,768]{1,0:T(8,128)(2,1)}, bf16[768,384]{1,0:T(8,128)(2,1)}, f32[8,768]{1,0:T(8,128)}, f32[8,1536]{1,0:T(8,128)}) custom-call(f32[768,768]{1,0:T(8,128)} %get-tuple-element.94.grad, bf16[768,768]{1,0:T(8,128)(2,1)} %get-tuple-element.95.mine, bf16[768,768]{1,0:T(8,128)(2,1)} %copy-done.11, ...), custom_call_target="tpu_custom_call" | custom-call | flops 452984832 | bytes 4000000 | tf_op jit(solution)/shard_map/branch/pallas_call | solution.py:501
  176.5 1.1 constant_dynamic-slice_fusion.2
  178.5 3.2 collective-permute-start.19
  182.5 35.0 %query_grads.1 = bf16[768,384]{1,0:T(8,128)(2,1)} custom-call(s32[7]{0:T(128)} %stack.48.s_ref.refs_0_, bf16[3072,1152]{1,0:T(8,128)(2,1)} %project_slots.3.q_ref.k_ref.v_ref.refs_1_.refs_2_.refs_3_, bf16[3072,1152]{1,0:T(8,128)(2,1)} %project_slots.3.q_ref.k_ref.v_ref.refs_1_.refs_2_.refs_3_, ...), custom_call_target="tpu_custom_call" | custom-call | flops 35999997952 | bytes 8000000 | tf_op jit(solution)/shard_map/query_grads/pallas_call | solution.py:205
  218.6 3.0 pad_maximum_fusion
  221.6 7.1 %collective-permute-start.15 = (bf16[208,3456]{1,0:T(8,128)(2,1)}, bf16[208,3456]{1,0:T(8,128)(2,1)S(1)}, u32[]{:S(2)}, u32[]{:S(2)}) collective-permute-start(bf16[208,3456]{1,0:T(8,128)(2,1)} %get-tuple-element.193), channel_id=1, source_target_pairs={{0,8},{8,0},{16,24},{24,16},{1,9},{9,1},{17,25},{25,17},{2,10},{10... | collective-permute-start | bytes 4313096 | tf_op jit(solution)/shard_map/ppermute | solution.py:613
  229.1 1.4 collective-permute-start.17
  234.6 1.0 collective-permute-done.23.refs_6_
  235.7 8.2 %project.1.refs_4_ = bf16[3072,384]{1,0:T(8,128)(2,1)} custom-call(s32[7]{0:T(128)} %stack.48.s_ref.refs_0_, bf16[768,768]{1,0:T(8,128)(2,1)} %get-tuple-element.106.refs_0_, bf16[416,768]{1,0:T(8,128)(2,1)} %collective-permute-done.18.refs_1_, bf16[416,768]{1,0:T(8,128)(2,1)} %copy-done.17, bf16[416,768]{1,0:T(8,128)(2,1)} %copy-done.13, ...), custom_call_target="tpu_custom_call" | custom-call | flops 1811939328 | bytes 4000000 | tf_op jit(solution)/shard_map/project/pallas_call | solution.py:385
  243.8 17.4 %collective-permute-done.15 = bf16[208,3456]{1,0:T(8,128)(2,1)S(1)} collective-permute-done((bf16[208,3456]{1,0:T(8,128)(2,1)}, bf16[208,3456]{1,0:T(8,128)(2,1)S(1)}, u32[]{:S(2)}, u32[]{:S(2)}) %collective-permute-start.15) | collective-permute-done | bytes 1437728 | tf_op jit(solution)/shard_map/ppermute | solution.py:613
  261.3 30.3 %collective-permute-done.16 = bf16[208,3456]{1,0:T(8,128)(2,1)S(1)} collective-permute-done((bf16[208,3456]{1,0:T(8,128)(2,1)}, bf16[208,3456]{1,0:T(8,128)(2,1)S(1)}, u32[]{:S(2)}, u32[]{:S(2)}) %collective-permute-start.16) | collective-permute-done | bytes 1437728 | tf_op jit(solution)/shard_map/ppermute | solution.py:613
  291.6 1.7 collective-permute-done.17
  294.3 12.8 %collective-permute-start.24 = (bf16[112,3456]{1,0:T(8,128)(2,1)S(1)}, bf16[112,3456]{1,0:T(8,128)(2,1)S(1)}, u32[]{:S(2)}, u32[]{:S(2)}) collective-permute-start(bf16[112,3456]{1,0:T(8,128)(2,1)S(1)} %pad_maximum_fusion.9), channel_id=1, source_target_pairs={{0,2},{2,0},{4,6},{6,4},{1,3},{3,1},{5,7},{7,5},{8,10},{10,8},{12,... | collective-permute-start | bytes 2322440 | tf_op jit(solution)/shard_map/ppermute | solution.py:613
  307.1 13.9 %key_grads.3 = (bf16[768,128]{1,0:T(8,128)(2,1)}, bf16[768,128]{1,0:T(8,128)(2,1)}) custom-call(s32[7]{0:T(128)} %stack.48.s_ref.refs_0_, bf16[3072,1152]{1,0:T(8,128)(2,1)} %project_slots.3.q_ref.k_ref.v_ref.refs_1_.refs_2_.refs_3_, bf16[3072,1152]{1,0:T(8,128)(2,1)} %project_slots.3.q_ref.k_ref.v_ref.refs_1_.refs_2_.refs_3_, ...), custom_call_target="tpu_custom_call" | custom-call | flops 14000000000 | bytes 4000000 | tf_op jit(solution)/shard_map/key_grads/pallas_call | solution.py:278
  321.0 1.0 constant_dynamic-update-slice_fusion.12
  322.0 2.1 collective-permute-done.24
  324.4 13.9 %key_grads.4 = (bf16[768,128]{1,0:T(8,128)(2,1)}, bf16[768,128]{1,0:T(8,128)(2,1)}) custom-call(s32[7]{0:T(128)} %stack.48.s_ref.refs_0_, bf16[3072,1152]{1,0:T(8,128)(2,1)} %project_slots.3.q_ref.k_ref.v_ref.refs_1_.refs_2_.refs_3_, bf16[3072,1152]{1,0:T(8,128)(2,1)} %project_slots.3.q_ref.k_ref.v_ref.refs_1_.refs_2_.refs_3_, ...), custom_call_target="tpu_custom_call" | custom-call | flops 14000000000 | bytes 4000000 | tf_op jit(solution)/shard_map/key_grads/pallas_call | solution.py:278
  338.2 14.0 %key_grads.5 = (bf16[768,128]{1,0:T(8,128)(2,1)}, bf16[768,128]{1,0:T(8,128)(2,1)}) custom-call(s32[7]{0:T(128)} %stack.48.s_ref.refs_0_, bf16[3072,1152]{1,0:T(8,128)(2,1)} %project_slots.3.q_ref.k_ref.v_ref.refs_1_.refs_2_.refs_3_, bf16[3072,1152]{1,0:T(8,128)(2,1)} %project_slots.3.q_ref.k_ref.v_ref.refs_1_.refs_2_.refs_3_, ...), custom_call_target="tpu_custom_call" | custom-call | flops 14000000000 | bytes 4000000 | tf_op jit(solution)/shard_map/key_grads/pallas_call | solution.py:278
  352.4 1.1 constant_dynamic-update-slice_fusion.15
  354.6 1.5 convolution_convert_fusion.2
  357.4 5.0 %collective-permute-start.29 = (bf16[208,256]{1,0:T(8,128)(2,1)S(1)}, bf16[208,256]{1,0:T(8,128)(2,1)S(1)}, u32[]{:S(2)}, u32[]{:S(2)}) collective-permute-start(bf16[208,256]{1,0:T(8,128)(2,1)S(1)} %get-tuple-element.205), channel_id=1, source_target_pairs={{0,8},{8,0},{16,24},{24,16},{1,9},{9,1},{17,25},{25,17},{2,10},{10... | collective-permute-start | bytes 319496 | tf_op jit(solution)/shard_map/ppermute | solution.py:613
  362.4 1.7 collective-permute-start.30
  364.6 1.8 collective-permute-start.26
  366.4 1.7 collective-permute-start.27
  368.6 1.2 collective-permute-start.28
  369.9 1.1 collective-permute-done.31
  371.0 6.7 %collective-permute-done.26 = bf16[208,896]{1,0:T(8,128)(2,1)S(1)} collective-permute-done((bf16[208,896]{1,0:T(8,128)(2,1)S(1)}, bf16[208,896]{1,0:T(8,128)(2,1)S(1)}, u32[]{:S(2)}, u32[]{:S(2)}) %collective-permute-start.26) | collective-permute-done | bytes 372768 | tf_op jit(solution)/shard_map/ppermute | solution.py:613
  377.7 7.7 %collective-permute-done.27 = bf16[208,896]{1,0:T(8,128)(2,1)S(1)} collective-permute-done((bf16[208,896]{1,0:T(8,128)(2,1)S(1)}, bf16[208,896]{1,0:T(8,128)(2,1)S(1)}, u32[]{:S(2)}, u32[]{:S(2)}) %collective-permute-start.27) | collective-permute-done | bytes 372768 | tf_op jit(solution)/shard_map/ppermute | solution.py:613
  385.8 11.3 %collective-permute-start.32 = (bf16[112,1152]{1,0:T(8,128)(2,1)S(1)}, bf16[112,1152]{1,0:T(8,128)(2,1)S(1)}, u32[]{:S(2)}, u32[]{:S(2)}) collective-permute-start(bf16[112,1152]{1,0:T(8,128)(2,1)S(1)} %maximum_maximum_fusion), channel_id=1, source_target_pairs={{0,2},{2,0},{4,6},{6,4},{1,3},{3,1},{5,7},{7,5},{8,10},{10,8},{12,... | collective-permute-start | bytes 774152 | tf_op jit(solution)/shard_map/ppermute | solution.py:613
  397.1 1.7 convolution_convert_fusion.3
  398.9 2.7 collective-permute-done.32
  401.8 2.6 collective-permute-start.33
  404.6 2.1 collective-permute-start.36
  408.5 5.8 %collective-permute-done.33 = bf16[112,1152]{1,0:T(8,128)(2,1)S(1)} collective-permute-done((bf16[112,1152]{1,0:T(8,128)(2,1)S(1)}, bf16[112,1152]{1,0:T(8,128)(2,1)S(1)}, u32[]{:S(2)}, u32[]{:S(2)}) %collective-permute-start.33) | collective-permute-done | bytes 258080 | tf_op jit(solution)/shard_map/ppermute | solution.py:613
  415.3 13.6 %collective-permute-done.34 = bf16[96,1152]{1,0:T(8,128)(2,1)S(1)} collective-permute-done((bf16[96,1152]{1,0:T(8,128)(2,1)S(1)}, bf16[96,1152]{1,0:T(8,128)(2,1)S(1)}, u32[]{:S(2)}, u32[]{:S(2)}) %collective-permute-start.34) | collective-permute-done | bytes 221216 | tf_op jit(solution)/shard_map/ppermute | solution.py:613
  431.1 1.4 add_convert_fusion.1
  432.7 1.7 convert_bitcast_fusion
  (213 shorter events, 30.8 us)
Async XLA Ops:
  1.8 26.4 %collective-permute-start.1 = (bf16[384,768]{1,0:T(8,128)(2,1)S(1)}, bf16[384,768]{1,0:T(8,128)(2,1)S(1)}, u32[]{:S(2)}, u32[]{:S(2)}) collective-permute-start(bf16[384,768]{1,0:T(8,128)(2,1)S(1)} %constant_dynamic-slice_fusion.15), channel_id=1, source_target_pairs={{0,2},{2,0},{4,6},{6,4},{1,3},{3,1},{5,7},{7,5},{8,10},{10,8},{12,... | collective-permute-start | bytes 1769480 | tf_op jit(solution)/shard_map/ppermute | solution.py:613
  4.9 23.3 %collective-permute-start.2 = (bf16[384,768]{1,0:T(8,128)(2,1)S(1)}, bf16[384,768]{1,0:T(8,128)(2,1)S(1)}, u32[]{:S(2)}, u32[]{:S(2)}) collective-permute-start(bf16[384,768]{1,0:T(8,128)(2,1)S(1)} %constant_dynamic-slice_fusion.15), channel_id=1, source_target_pairs={{2,4},{4,2},{3,5},{5,3},{10,12},{12,10},{11,13},{13,11},{18,20},{2... | collective-permute-start | bytes 1769480 | tf_op jit(solution)/shard_map/ppermute | solution.py:645
  5.6 13.3 %collective-permute-start.3 = (bf16[3,192,384]{2,1,0:T(8,128)(2,1)}, bf16[3,192,384]{2,1,0:T(8,128)(2,1)S(1)}, u32[]{:S(2)}, u32[]{:S(2)}) collective-permute-start(bf16[3,192,384]{2,1,0:T(8,128)(2,1)} %refs_5_), channel_id=1, source_target_pairs={{0,8},{8,0},{16,24},{24,16},{1,9},{9,1},{17,25},{25,17},{2,10},{10... | collective-permute-start | bytes 1327112 | tf_op jit(solution)/shard_map/ppermute | solution.py:613
  7.1 21.0 %collective-permute-start.4 = (bf16[3,192,384]{2,1,0:T(8,128)(2,1)}, bf16[3,192,384]{2,1,0:T(8,128)(2,1)S(1)}, u32[]{:S(2)}, u32[]{:S(2)}) collective-permute-start(bf16[3,192,384]{2,1,0:T(8,128)(2,1)} %refs_5_), channel_id=1, source_target_pairs={{0,16},{8,24},{16,0},{24,8},{1,17},{9,25},{17,1},{25,9},{2,18},{10... | collective-permute-start | bytes 1327112 | tf_op jit(solution)/shard_map/ppermute | solution.py:613
  8.6 19.5 %collective-permute-start.5 = (bf16[3,192,384]{2,1,0:T(8,128)(2,1)}, bf16[3,192,384]{2,1,0:T(8,128)(2,1)S(1)}, u32[]{:S(2)}, u32[]{:S(2)}) collective-permute-start(bf16[3,192,384]{2,1,0:T(8,128)(2,1)} %refs_5_), channel_id=1, source_target_pairs={{0,24},{8,16},{16,8},{24,0},{1,25},{9,17},{17,9},{25,1},{2,26},{10... | collective-permute-start | bytes 1327112 | tf_op jit(solution)/shard_map/ppermute | solution.py:613
  18.9 9.4 %copy-start.43 = (bf16[3,192,384]{2,1,0:T(8,128)(2,1)}, bf16[3,192,384]{2,1,0:T(8,128)(2,1)S(1)}, u32[]{:S(2)}) copy-start(bf16[3,192,384]{2,1,0:T(8,128)(2,1)S(1)} %collective-permute-done.3.refs_6_) | copy-start | bytes 1327108
  28.2 10.1 %copy-start.39 = (bf16[384,768]{1,0:T(8,128)(2,1)}, bf16[384,768]{1,0:T(8,128)(2,1)S(1)}, u32[]{:S(2)}) copy-start(bf16[384,768]{1,0:T(8,128)(2,1)S(1)} %collective-permute-done.1.refs_1_) | copy-start | bytes 1769476
  28.2 10.1 %copy-start.40 = (bf16[384,768]{1,0:T(8,128)(2,1)}, bf16[384,768]{1,0:T(8,128)(2,1)S(1)}, u32[]{:S(2)}) copy-start(bf16[384,768]{1,0:T(8,128)(2,1)S(1)} %collective-permute-done.2.refs_3_) | copy-start | bytes 1769476
  28.2 10.1 %collective-permute-start.6 = (bf16[384,768]{1,0:T(8,128)(2,1)S(1)}, bf16[384,768]{1,0:T(8,128)(2,1)S(1)}, u32[]{:S(2)}, u32[]{:S(2)}) collective-permute-start(bf16[384,768]{1,0:T(8,128)(2,1)S(1)} %collective-permute-done.1.refs_1_), channel_id=1, source_target_pairs={{0,1},{1,0},{2,3},{3,2},{4,5},{5,4},{6,7},{7,6},{8,9},{9,8},{10,11... | collective-permute-start | bytes 1769480 | tf_op jit(solution)/shard_map/ppermute | solution.py:616
  28.3 10.0 %collective-permute-start.7 = (bf16[384,768]{1,0:T(8,128)(2,1)S(1)}, bf16[384,768]{1,0:T(8,128)(2,1)S(1)}, u32[]{:S(2)}, u32[]{:S(2)}) collective-permute-start(bf16[384,768]{1,0:T(8,128)(2,1)S(1)} %collective-permute-done.2.refs_3_), channel_id=1, source_target_pairs={{0,1},{1,0},{2,3},{3,2},{4,5},{5,4},{6,7},{7,6},{8,9},{9,8},{10,11... | collective-permute-start | bytes 1769480 | tf_op jit(solution)/shard_map/ppermute | solution.py:616
  29.2 29.6 %collective-permute-start = (bf16[384,768]{1,0:T(8,128)(2,1)S(1)}, bf16[384,768]{1,0:T(8,128)(2,1)S(1)}, u32[]{:S(2)}, u32[]{:S(2)}) collective-permute-start(bf16[384,768]{1,0:T(8,128)(2,1)S(1)} %constant_dynamic-slice_fusion.15), channel_id=1, source_target_pairs={{0,4},{2,6},{4,0},{6,2},{1,5},{3,7},{5,1},{7,3},{8,12},{10,14},{12... | collective-permute-start | bytes 1769480 | tf_op jit(solution)/shard_map/ppermute | solution.py:613
  38.3 20.6 %copy-start.34 = (s32[3072]{0:T(1024)S(1)}, s32[3072]{0:T(1024)}, u32[]{:S(2)}) copy-start(s32[3072]{0:T(1024)} %param.23) | copy-start | bytes 36868
  38.3 21.2 %copy-start.22 = (bf16[1536,192]{0,1:T(8,128)(2,1)S(1)}, bf16[1536,192]{0,1:T(8,128)(2,1)}, u32[]{:S(2)}) copy-start(bf16[1536,192]{0,1:T(8,128)(2,1)} %param.19) | copy-start | bytes 1769476
  38.3 21.2 %copy-start.23 = (bf16[192,1536]{1,0:T(8,128)(2,1)S(1)}, bf16[192,1536]{1,0:T(8,128)(2,1)}, u32[]{:S(2)}) copy-start(bf16[192,1536]{1,0:T(8,128)(2,1)} %param.17) | copy-start | bytes 1769476
  38.3 21.2 %copy-start.32 = (bf16[384,192]{0,1:T(8,128)(2,1)S(1)}, bf16[384,192]{0,1:T(8,128)(2,1)}, u32[]{:S(2)}) copy-start(bf16[384,192]{0,1:T(8,128)(2,1)} %param.16) | copy-start | bytes 442372
  58.8 4.3 copy-start.19
  58.8 4.3 collective-permute-start.8
  59.6 9.9 %copy-start = (bf16[192,3456]{1,0:T(8,128)(2,1)}, bf16[192,3456]{1,0:T(8,128)(2,1)S(1)}, u32[]{:S(2)}) copy-start(bf16[192,3456]{1,0:T(8,128)(2,1)S(1)} %pad_maximum_fusion.6.refs_0_) | copy-start | bytes 3981316
  59.6 60.0 %collective-permute-start.10 = (bf16[192,3456]{1,0:T(8,128)(2,1)S(1)}, bf16[192,3456]{1,0:T(8,128)(2,1)S(1)}, u32[]{:S(2)}, u32[]{:S(2)}) collective-permute-start(bf16[192,3456]{1,0:T(8,128)(2,1)S(1)} %pad_maximum_fusion.6.refs_0_), channel_id=1, source_target_pairs={{0,16},{8,24},{16,0},{24,8},{1,17},{9,25},{17,1},{25,9},{2,18},{10... | collective-permute-start | bytes 3981320 | tf_op jit(solution)/shard_map/ppermute | solution.py:613
  61.2 58.4 %collective-permute-start.11 = (bf16[192,3456]{1,0:T(8,128)(2,1)S(1)}, bf16[192,3456]{1,0:T(8,128)(2,1)S(1)}, u32[]{:S(2)}, u32[]{:S(2)}) collective-permute-start(bf16[192,3456]{1,0:T(8,128)(2,1)S(1)} %pad_maximum_fusion.6.refs_0_), channel_id=1, source_target_pairs={{0,24},{8,16},{16,8},{24,0},{1,25},{9,17},{17,9},{25,1},{2,26},{10... | collective-permute-start | bytes 3981320 | tf_op jit(solution)/shard_map/ppermute | solution.py:613
  62.3 58.5 %collective-permute-start.9 = (bf16[192,3456]{1,0:T(8,128)(2,1)S(1)}, bf16[192,3456]{1,0:T(8,128)(2,1)S(1)}, u32[]{:S(2)}, u32[]{:S(2)}) collective-permute-start(bf16[192,3456]{1,0:T(8,128)(2,1)S(1)} %pad_maximum_fusion.6.refs_0_), channel_id=1, source_target_pairs={{0,8},{8,0},{16,24},{24,16},{1,9},{9,1},{17,25},{25,17},{2,10},{10... | collective-permute-start | bytes 3981320 | tf_op jit(solution)/shard_map/ppermute | solution.py:613
  121.9 6.0 %copy-start.3 = (bf16[768,384]{1,0:T(8,128)(2,1)S(1)}, bf16[768,384]{1,0:T(8,128)(2,1)}, u32[]{:S(2)}) copy-start(bf16[768,384]{1,0:T(8,128)(2,1)} %get-tuple-element.81.att) | copy-start | bytes 1769476
  129.7 2.9 copy-start.12
  129.7 2.9 collective-permute-start.12
  133.7 11.8 %copy-start.33 = (f32[8,768]{1,0:T(8,128)S(1)}, f32[8,768]{1,0:T(8,128)}, u32[]{:S(2)}) copy-start(f32[8,768]{1,0:T(8,128)} %get-tuple-element.100) | copy-start | bytes 73732
  144.6 3.1 collective-permute-start.13
  148.7 12.7 %copy-start.46 = (bf16[768,1536]{1,0:T(8,128)(2,1)S(1)}, bf16[768,1536]{1,0:T(8,128)(2,1)}, u32[]{:S(2)}) copy-start(bf16[768,1536]{1,0:T(8,128)(2,1)} %get-tuple-element.103) | copy-start | bytes 7077892
  161.2 6.0 %collective-permute-start.14 = (bf16[768,768]{1,0:T(8,128)(2,1)}, bf16[768,768]{1,0:T(8,128)(2,1)S(1)}, u32[]{:S(2)}, u32[]{:S(2)}) collective-permute-start(bf16[768,768]{1,0:T(8,128)(2,1)} %get-tuple-element.95.mine), channel_id=1, source_target_pairs={{0,1},{1,0},{2,3},{3,2},{4,5},{5,4},{6,7},{7,6},{8,9},{9,8},{10,11... | collective-permute-start | bytes 3538952 | tf_op jit(solution)/shard_map/ppermute | solution.py:616
  161.4 3.5 copy-start.37
  161.4 3.5 copy-start.47
  176.5 5.9 %copy-start.24 = (f32[16,768]{1,0:T(8,128)}, f32[16,768]{1,0:T(8,128)S(1)}, u32[]{:S(2)}) copy-start(f32[16,768]{1,0:T(8,128)S(1)} %constant_dynamic-update-slice_fusion.stat_ref) | copy-start | bytes 147460
  178.5 39.9 %collective-permute-start.18 = (bf16[416,768]{1,0:T(8,128)(2,1)}, bf16[416,768]{1,0:T(8,128)(2,1)}, u32[]{:S(2)}, u32[]{:S(2)}) collective-permute-start(bf16[416,768]{1,0:T(8,128)(2,1)} %pad_maximum_fusion.17), channel_id=1, source_target_pairs={{0,2},{2,0},{4,6},{6,4},{1,3},{3,1},{5,7},{7,5},{8,10},{10,8},{12,... | collective-permute-start | bytes 1916936 | tf_op jit(solution)/shard_map/ppermute | solution.py:613
  178.5 39.9 %collective-permute-start.19 = (bf16[416,768]{1,0:T(8,128)(2,1)}, bf16[416,768]{1,0:T(8,128)(2,1)S(1)}, u32[]{:S(2)}, u32[]{:S(2)}) collective-permute-start(bf16[416,768]{1,0:T(8,128)(2,1)} %pad_maximum_fusion.17), channel_id=1, source_target_pairs={{0,4},{2,6},{4,0},{6,2},{1,5},{3,7},{5,1},{7,3},{8,12},{10,14},{12... | collective-permute-start | bytes 1916936 | tf_op jit(solution)/shard_map/ppermute | solution.py:613
  181.7 36.7 %collective-permute-start.20 = (bf16[416,768]{1,0:T(8,128)(2,1)}, bf16[416,768]{1,0:T(8,128)(2,1)S(1)}, u32[]{:S(2)}, u32[]{:S(2)}) collective-permute-start(bf16[416,768]{1,0:T(8,128)(2,1)} %pad_maximum_fusion.17), channel_id=1, source_target_pairs={{2,4},{4,2},{3,5},{5,3},{10,12},{12,10},{11,13},{13,11},{18,20},{2... | collective-permute-start | bytes 1916936 | tf_op jit(solution)/shard_map/ppermute | solution.py:645
  182.4 35.1 %copy-start.2 = (bf16[768,768]{1,0:T(8,128)(2,1)S(1)}, bf16[768,768]{1,0:T(8,128)(2,1)}, u32[]{:S(2)}) copy-start(bf16[768,768]{1,0:T(8,128)(2,1)} %get-tuple-element.106.refs_0_) | copy-start | bytes 3538948
  182.5 35.1 %copy-start.4 = (bf16[768,384]{1,0:T(8,128)(2,1)S(1)}, bf16[768,384]{1,0:T(8,128)(2,1)}, u32[]{:S(2)}) copy-start(bf16[768,384]{1,0:T(8,128)(2,1)} %get-tuple-element.81.att) | copy-start | bytes 1769476
  218.5 3.1 copy-start.13
  218.5 3.1 copy-start.15
  218.5 14.0 %collective-permute-start.21 = (bf16[416,768]{1,0:T(8,128)(2,1)}, bf16[416,768]{1,0:T(8,128)(2,1)S(1)}, u32[]{:S(2)}, u32[]{:S(2)}) collective-permute-start(bf16[416,768]{1,0:T(8,128)(2,1)} %collective-permute-done.18.refs_1_), channel_id=1, source_target_pairs={{0,1},{1,0},{2,3},{3,2},{4,5},{5,4},{6,7},{7,6},{8,9},{9,8},{10,11... | collective-permute-start | bytes 1916936 | tf_op jit(solution)/shard_map/ppermute | solution.py:616
  218.6 11.9 %copy-start.21 = (bf16[768,384]{1,0:T(8,128)(2,1)S(1)}, bf16[768,384]{1,0:T(8,128)(2,1)}, u32[]{:S(2)}) copy-start(bf16[768,384]{1,0:T(8,128)(2,1)} %query_grads.1) | copy-start | bytes 1769476
  221.6 39.7 %collective-permute-start.15 = (bf16[208,3456]{1,0:T(8,128)(2,1)}, bf16[208,3456]{1,0:T(8,128)(2,1)S(1)}, u32[]{:S(2)}, u32[]{:S(2)}) collective-permute-start(bf16[208,3456]{1,0:T(8,128)(2,1)} %get-tuple-element.193), channel_id=1, source_target_pairs={{0,8},{8,0},{16,24},{24,16},{1,9},{9,1},{17,25},{25,17},{2,10},{10... | collective-permute-start | bytes 4313096 | tf_op jit(solution)/shard_map/ppermute | solution.py:613
  228.7 62.9 %collective-permute-start.16 = (bf16[208,3456]{1,0:T(8,128)(2,1)}, bf16[208,3456]{1,0:T(8,128)(2,1)S(1)}, u32[]{:S(2)}, u32[]{:S(2)}) collective-permute-start(bf16[208,3456]{1,0:T(8,128)(2,1)} %get-tuple-element.192), channel_id=1, source_target_pairs={{0,16},{8,24},{16,0},{24,8},{1,17},{9,25},{17,1},{25,9},{2,18},{10... | collective-permute-start | bytes 4313096 | tf_op jit(solution)/shard_map/ppermute | solution.py:613
  229.1 64.2 %collective-permute-start.17 = (bf16[208,3456]{1,0:T(8,128)(2,1)}, bf16[208,3456]{1,0:T(8,128)(2,1)S(1)}, u32[]{:S(2)}, u32[]{:S(2)}) collective-permute-start(bf16[208,3456]{1,0:T(8,128)(2,1)} %get-tuple-element.191), channel_id=1, source_target_pairs={{0,24},{8,16},{16,8},{24,0},{1,25},{9,17},{17,9},{25,1},{2,26},{10... | collective-permute-start | bytes 4313096 | tf_op jit(solution)/shard_map/ppermute | solution.py:613
  231.5 2.4 copy-start.25
  232.5 2.1 collective-permute-start.22
  232.7 2.9 collective-permute-start.23
  294.3 26.7 %copy-start.26 = (bf16[768,1152]{1,0:T(8,128)(2,1)S(1)}, bf16[768,1152]{1,0:T(8,128)(2,1)}, u32[]{:S(2)}) copy-start(bf16[768,1152]{1,0:T(8,128)(2,1)} %get-tuple-element.161) | copy-start | bytes 5308420
  294.3 29.8 %collective-permute-start.24 = (bf16[112,3456]{1,0:T(8,128)(2,1)S(1)}, bf16[112,3456]{1,0:T(8,128)(2,1)S(1)}, u32[]{:S(2)}, u32[]{:S(2)}) collective-permute-start(bf16[112,3456]{1,0:T(8,128)(2,1)S(1)} %pad_maximum_fusion.9), channel_id=1, source_target_pairs={{0,2},{2,0},{4,6},{6,4},{1,3},{3,1},{5,7},{7,5},{8,10},{10,8},{12,... | collective-permute-start | bytes 2322440 | tf_op jit(solution)/shard_map/ppermute | solution.py:613
  338.2 14.0 %copy-start.31 = (bf16[768,128]{1,0:T(8,128)(2,1)S(1)}, bf16[768,128]{1,0:T(8,128)(2,1)}, u32[]{:S(2)}) copy-start(bf16[768,128]{1,0:T(8,128)(2,1)} %get-tuple-element.121) | copy-start | bytes 589828
  338.2 15.3 %copy-start.28 = (bf16[768,128]{1,0:T(8,128)(2,1)S(1)}, bf16[768,128]{1,0:T(8,128)(2,1)}, u32[]{:S(2)}) copy-start(bf16[768,128]{1,0:T(8,128)(2,1)} %get-tuple-element.124) | copy-start | bytes 589828
  356.4 48.0 %collective-permute-start.35 = (bf16[112,3456]{1,0:T(8,128)(2,1)S(1)}, bf16[112,3456]{1,0:T(8,128)(2,1)S(1)}, u32[]{:S(2)}, u32[]{:S(2)}) collective-permute-start(bf16[112,3456]{1,0:T(8,128)(2,1)S(1)} %pad_maximum_fusion.10), channel_id=1, source_target_pairs={{0,4},{2,6},{4,0},{6,2},{1,5},{3,7},{5,1},{7,3},{8,12},{10,14},{12... | collective-permute-start | bytes 2322440 | tf_op jit(solution)/shard_map/ppermute | solution.py:613
  357.4 8.9 %collective-permute-start.29 = (bf16[208,256]{1,0:T(8,128)(2,1)S(1)}, bf16[208,256]{1,0:T(8,128)(2,1)S(1)}, u32[]{:S(2)}, u32[]{:S(2)}) collective-permute-start(bf16[208,256]{1,0:T(8,128)(2,1)S(1)} %get-tuple-element.205), channel_id=1, source_target_pairs={{0,8},{8,0},{16,24},{24,16},{1,9},{9,1},{17,25},{25,17},{2,10},{10... | collective-permute-start | bytes 319496 | tf_op jit(solution)/shard_map/ppermute | solution.py:613
  362.4 6.2 %collective-permute-start.30 = (bf16[208,256]{1,0:T(8,128)(2,1)S(1)}, bf16[208,256]{1,0:T(8,128)(2,1)S(1)}, u32[]{:S(2)}, u32[]{:S(2)}) collective-permute-start(bf16[208,256]{1,0:T(8,128)(2,1)S(1)} %get-tuple-element.206), channel_id=1, source_target_pairs={{0,16},{8,24},{16,0},{24,8},{1,17},{9,25},{17,1},{25,9},{2,18},{10... | collective-permute-start | bytes 319496 | tf_op jit(solution)/shard_map/ppermute | solution.py:613
  364.2 6.7 %collective-permute-start.31 = (bf16[208,256]{1,0:T(8,128)(2,1)S(1)}, bf16[208,256]{1,0:T(8,128)(2,1)S(1)}, u32[]{:S(2)}, u32[]{:S(2)}) collective-permute-start(bf16[208,256]{1,0:T(8,128)(2,1)S(1)} %get-tuple-element.207), channel_id=1, source_target_pairs={{0,24},{8,16},{16,8},{24,0},{1,25},{9,17},{17,9},{25,1},{2,26},{10... | collective-permute-start | bytes 319496 | tf_op jit(solution)/shard_map/ppermute | solution.py:613
  364.6 13.2 %collective-permute-start.26 = (bf16[208,896]{1,0:T(8,128)(2,1)S(1)}, bf16[208,896]{1,0:T(8,128)(2,1)S(1)}, u32[]{:S(2)}, u32[]{:S(2)}) collective-permute-start(bf16[208,896]{1,0:T(8,128)(2,1)S(1)} %get-tuple-element.200), channel_id=1, source_target_pairs={{0,8},{8,0},{16,24},{24,16},{1,9},{9,1},{17,25},{25,17},{2,10},{10... | collective-permute-start | bytes 1118216 | tf_op jit(solution)/shard_map/ppermute | solution.py:613
  366.4 19.0 %collective-permute-start.27 = (bf16[208,896]{1,0:T(8,128)(2,1)S(1)}, bf16[208,896]{1,0:T(8,128)(2,1)S(1)}, u32[]{:S(2)}, u32[]{:S(2)}) collective-permute-start(bf16[208,896]{1,0:T(8,128)(2,1)S(1)} %get-tuple-element.199), channel_id=1, source_target_pairs={{0,16},{8,24},{16,0},{24,8},{1,17},{9,25},{17,1},{25,9},{2,18},{10... | collective-permute-start | bytes 1118216 | tf_op jit(solution)/shard_map/ppermute | solution.py:613
  368.6 16.8 %collective-permute-start.28 = (bf16[208,896]{1,0:T(8,128)(2,1)S(1)}, bf16[208,896]{1,0:T(8,128)(2,1)S(1)}, u32[]{:S(2)}, u32[]{:S(2)}) collective-permute-start(bf16[208,896]{1,0:T(8,128)(2,1)S(1)} %get-tuple-element.198), channel_id=1, source_target_pairs={{0,24},{8,16},{16,8},{24,0},{1,25},{9,17},{17,9},{25,1},{2,26},{10... | collective-permute-start | bytes 1118216 | tf_op jit(solution)/shard_map/ppermute | solution.py:613
  385.4 11.6 %copy-start.6 = (bf16[768,1152]{1,0:T(8,128)(2,1)S(1)}, bf16[768,1152]{1,0:T(8,128)(2,1)}, u32[]{:S(2)}) copy-start(bf16[768,1152]{1,0:T(8,128)(2,1)} %get-tuple-element.78.refs_2_) | copy-start | bytes 5308420
  385.8 15.8 %collective-permute-start.32 = (bf16[112,1152]{1,0:T(8,128)(2,1)S(1)}, bf16[112,1152]{1,0:T(8,128)(2,1)S(1)}, u32[]{:S(2)}, u32[]{:S(2)}) collective-permute-start(bf16[112,1152]{1,0:T(8,128)(2,1)S(1)} %maximum_maximum_fusion), channel_id=1, source_target_pairs={{0,2},{2,0},{4,6},{6,4},{1,3},{3,1},{5,7},{7,5},{8,10},{10,8},{12,... | collective-permute-start | bytes 774152 | tf_op jit(solution)/shard_map/ppermute | solution.py:613
  398.8 31.4 %collective-permute-start.25 = (bf16[768,768]{1,0:T(8,128)(2,1)S(1)}, bf16[768,768]{1,0:T(8,128)(2,1)S(1)}, u32[]{:S(2)}, u32[]{:S(2)}) collective-permute-start(bf16[768,768]{1,0:T(8,128)(2,1)S(1)} %convolution_convert_fusion.3), channel_id=1, source_target_pairs={{0,1},{1,0},{2,3},{3,2},{4,5},{5,4},{6,7},{7,6},{8,9},{9,8},{10,11... | collective-permute-start | bytes 3538952 | tf_op jit(solution)/shard_map/ppermute | solution.py:616
  401.8 12.6 %collective-permute-start.33 = (bf16[112,1152]{1,0:T(8,128)(2,1)S(1)}, bf16[112,1152]{1,0:T(8,128)(2,1)S(1)}, u32[]{:S(2)}, u32[]{:S(2)}) collective-permute-start(bf16[112,1152]{1,0:T(8,128)(2,1)S(1)} %maximum_maximum_fusion.1), channel_id=1, source_target_pairs={{0,4},{2,6},{4,0},{6,2},{1,5},{3,7},{5,1},{7,3},{8,12},{10,14},{12... | collective-permute-start | bytes 774152 | tf_op jit(solution)/shard_map/ppermute | solution.py:613
  404.6 27.9 %collective-permute-start.36 = (bf16[96,3456]{1,0:T(8,128)(2,1)S(1)}, bf16[96,3456]{1,0:T(8,128)(2,1)S(1)}, u32[]{:S(2)}, u32[]{:S(2)}) collective-permute-start(bf16[96,3456]{1,0:T(8,128)(2,1)S(1)} %add_convert_fusion.2), channel_id=1, source_target_pairs={{0,2},{2,0},{4,6},{6,4},{1,3},{3,1},{5,7},{7,5},{8,10},{10,8},{12,... | collective-permute-start | bytes 1990664 | tf_op jit(solution)/shard_map/ppermute | solution.py:613
  414.4 14.5 %collective-permute-start.34 = (bf16[96,1152]{1,0:T(8,128)(2,1)S(1)}, bf16[96,1152]{1,0:T(8,128)(2,1)S(1)}, u32[]{:S(2)}, u32[]{:S(2)}) collective-permute-start(bf16[96,1152]{1,0:T(8,128)(2,1)S(1)} %add_convert_fusion.5), channel_id=1, source_target_pairs={{0,2},{2,0},{4,6},{6,4},{1,3},{3,1},{5,7},{7,5},{8,10},{10,8},{12,... | collective-permute-start | bytes 663560 | tf_op jit(solution)/shard_map/ppermute | solution.py:613
  429.1 2.0 copy-start.5
  (21 other events, 25.0 us)
